TPU v7x, 32 devices: a whole 2x2x4 slice. The times are simulated.
32 devices in a mesh: head: 4 (over z), node: 8 (over y, x, core).
Axes of the slice: x: 2, y: 2, z: 4, core: 2. Of those that a mesh axis runs over, the one named last changes fastest.
Arguments:
- node_input: bfloat16 [8192, 512], P('node'), may hold values from -6 to 6
- cotangent: bfloat16 [8192, 512], P('node'), may hold values from -6 to 6
- sigma_embed: bfloat16 [4, 512], replicated, may hold values from -5 to 5
- neighbours: int32 [8192, 16], P('node'), may hold values from 0 to 8191, as said below
- neighbour_valid: int32 [8192, 16], P('node'), may hold values 0 or 1
- batch_counts: int32 [4], replicated, may hold values from 1 to 4096, 8192 in all
- step_count: int32 [1], replicated, may hold values from 1 to 20
- ada_master: float32 [512, 2048], P('node'), may hold values from -0.125 to 0.125
- ada_first: float32 [512, 2048], P('node'), may hold values from -768 to 768
- ada_second: float32 [512, 2048], P('node'), may hold values from 16384 to 65536
- qkv_master: float32 [512, 1536], P('node', 'head'), may hold values from -0.375 to 0.375
- qkv_first: float32 [512, 1536], P('node', 'head'), may hold values from -1024 to 1024
- qkv_second: float32 [512, 1536], P('node', 'head'), may hold values from 32768 to 131072
- out_master: float32 [512, 512], P(('head', 'node')), may hold values from -0.5 to 0.5
- out_first: float32 [512, 512], P(('head', 'node')), may hold values from -384 to 384
- out_second: float32 [512, 512], P(('head', 'node')), may hold values from 4096 to 16384
- up_master: float32 [512, 2048], P('node', 'head'), may hold values from -0.25 to 0.25
- up_first: float32 [512, 2048], P('node', 'head'), may hold values from -128 to 128
- up_second: float32 [512, 2048], P('node', 'head'), may hold values from 491.52 to 2048
- down_master: float32 [2048, 512], P(('head', 'node')), may hold values from -0.125 to 0.125
- down_first: float32 [2048, 512], P(('head', 'node')), may hold values from -256 to 256
- down_second: float32 [2048, 512], P(('head', 'node')), may hold values from 2048 to 8192
Outputs:
- node_output: bfloat16 [8192, 512], P('node')
- input_grad: float32 [8192, 512], P('node')
- ada_new: float32 [512, 2048], P('node')
- ada_first_new: float32 [512, 2048], P('node')
- ada_second_new: float32 [512, 2048], P('node')
- qkv_new: float32 [512, 1536], P('node', 'head')
- qkv_first_new: float32 [512, 1536], P('node', 'head')
- qkv_second_new: float32 [512, 1536], P('node', 'head')
- out_new: float32 [512, 512], P(('head', 'node'))
- out_first_new: float32 [512, 512], P(('head', 'node'))
- out_second_new: float32 [512, 512], P(('head', 'node'))
- up_new: float32 [512, 2048], P('node', 'head')
- up_first_new: float32 [512, 2048], P('node', 'head')
- up_second_new: float32 [512, 2048], P('node', 'head')
- down_new: float32 [2048, 512], P(('head', 'node'))
- down_first_new: float32 [2048, 512], P(('head', 'node'))
- down_second_new: float32 [2048, 512], P(('head', 'node'))
Inputs may be any that keep to these rules, and one draw needn't show every extreme that they name: `batch_counts`: the counts sum to 8192; the largest is exactly 4096. Node n's neighbours lie in its own aligned block of 1024 nodes or in the two blocks on either side of it, counted cyclically over the 8192 nodes.
All inputs are finite; a program needn't handle non-finite values. No bound on the sum of `neighbour_valid` on one device may be relied on, other than what follows from the above.
Results may differ from a plain program's by a relative error of at most 0.018.
The roundings to bfloat16 on the way count: a program that leaves them out, or rounds other values in their place, can miss the bound.
Values may be sent and summed in bfloat16 or wider, within the bound.
A program may use at most 128 MiB of HBM per device.

v0:
```python
import jax
import jax.numpy as jnp
from jax import lax
from jax.sharding import PartitionSpec as P

WIDTH = 512
HIDDEN_SIZE = 2048
COND = 512


norm_eps = 1e-06
beta_rate = 0.5
adam_eps = 1e-08
weight_decay = 0.1
highest = lax.Precision.HIGHEST


def passed_along(block, axis, distance):
    devices = range(lax.axis_size(axis))
    route = [((i - distance) % len(devices), i) for i in devices]
    return lax.ppermute(block, axis, route)


def norm_parts(values):
    centred = values - jnp.mean(values, axis=1, keepdims=True)
    inverse = lax.rsqrt(jnp.mean(centred * centred, axis=1, keepdims=True) + norm_eps)
    return (centred * inverse, inverse)


def norm_back(grad_normed, normed, inverse):
    first_mean = jnp.mean(grad_normed, axis=1, keepdims=True)
    second_mean = jnp.mean(grad_normed * normed, axis=1, keepdims=True)
    return inverse * (grad_normed - first_mean - normed * second_mean)


def adamw_update(master, first, second, grad, rate, count_value):
    first_new = beta_rate * first + (1.0 - beta_rate) * grad
    second_new = beta_rate * second + (1.0 - beta_rate) * grad * grad
    correct = 1.0 - jnp.power(jnp.float32(beta_rate), count_value)
    normed_step = first_new / correct / (jnp.sqrt(second_new / correct) + adam_eps)
    master_new = master - rate * (normed_step + weight_decay * master)
    return (master_new, first_new, second_new)


def per_device(
    node_input,
    cotangent,
    sigma_embed,
    neighbours,
    neighbour_valid,
    batch_counts,
    step_count,
    ada_master,
    ada_first,
    ada_second,
    qkv_master,
    qkv_first,
    qkv_second,
    out_master,
    out_first,
    out_second,
    up_master,
    up_first,
    up_second,
    down_master,
    down_first,
    down_second,
):
    f32 = jnp.float32
    bf16 = jnp.bfloat16
    node_rows = node_input.shape[0]
    model_width = node_input.shape[1]
    head_dim = qkv_master.shape[1] // 3
    score_scale = head_dim ** (-0.5)
    node_index = lax.axis_index("node")
    total_nodes = node_rows * lax.axis_size("node")
    ada_full, qkv_full, out_full, up_full, down_full = (
        lax.all_gather(ada_master.astype(bf16), "node", axis=0, tiled=True),
        lax.all_gather(qkv_master.astype(bf16), "node", axis=0, tiled=True),
        lax.all_gather(out_master.astype(bf16), "node", axis=0, tiled=True),
        lax.all_gather(up_master.astype(bf16), "node", axis=0, tiled=True),
        lax.all_gather(down_master.astype(bf16), "node", axis=0, tiled=True),
    )
    limits = jnp.cumsum(batch_counts)[:-1]
    positions = node_index * node_rows + jnp.arange(node_rows, dtype=jnp.int32)
    member = jnp.sum((positions[:, None] >= limits[None, :]).astype(jnp.int32), axis=1)
    onehot = (
        member[:, None] == jnp.arange(batch_counts.shape[0], dtype=jnp.int32)[None, :]
    ).astype(f32)
    modulation = jnp.dot(sigma_embed, ada_full, preferred_element_type=f32)
    per_node = jnp.dot(onehot, modulation, precision=highest)
    scale_one = per_node[:, :model_width]
    shift_one = per_node[:, model_width : 2 * model_width]
    scale_two = per_node[:, 2 * model_width : 3 * model_width]
    shift_two = per_node[:, 3 * model_width :]
    normed_one, inverse_one = norm_parts(node_input.astype(f32))
    xn_one = (normed_one * (1.0 + scale_one) + shift_one).astype(bf16)
    projected = jnp.dot(xn_one, qkv_full, preferred_element_type=f32).astype(bf16)
    queries = projected[:, :head_dim]
    keys_values = projected[:, head_dim:]
    key_rows = keys_values[:, :head_dim]
    value_rows = keys_values[:, head_dim:]
    offsets = (-2, -1, 1, 2)
    fetched = {0: keys_values}
    for offset in offsets:
        fetched[offset] = passed_along(keys_values, "node", -offset)
    table_rows = jnp.concatenate([fetched[offset] for offset in (-2, -1, 0, 1, 2)], axis=0)
    slot_index = jnp.mod(neighbours - (node_index - 2) * node_rows, total_nodes)
    near_rows = table_rows[slot_index]
    near_keys = near_rows[:, :, :head_dim]
    near_values = near_rows[:, :, head_dim:]
    is_valid = neighbour_valid > 0
    queries_f = queries.astype(f32)
    keys_f = key_rows.astype(f32)
    values_f = value_rows.astype(f32)
    near_values_f = near_values.astype(f32)
    self_score = jnp.sum(queries_f * keys_f, axis=1) * score_scale
    near_score = (
        jnp.einsum("nd,nkd->nk", queries, near_keys, preferred_element_type=f32) * score_scale
    )
    near_score = jnp.where(is_valid, near_score, -1e30)
    row_max = jnp.maximum(jnp.max(near_score, axis=1), self_score)
    self_exp = jnp.exp(self_score - row_max)
    near_exp = jnp.exp(near_score - row_max[:, None])
    denominator = self_exp + jnp.sum(near_exp, axis=1)
    self_prob = self_exp / denominator
    near_prob = near_exp / denominator[:, None]
    mixed = self_prob[:, None] * values_f + jnp.einsum("nk,nkd->nd", near_prob, near_values_f)
    heads_out = mixed.astype(bf16)
    branch = lax.psum(
        jnp.dot(heads_out, out_full, preferred_element_type=f32).astype(jnp.bfloat16), "head"
    ).astype(jnp.float32)
    middle = node_input.astype(f32) + branch
    normed_two, inverse_two = norm_parts(middle)
    xn_two = (normed_two * (1.0 + scale_two) + shift_two).astype(bf16)
    hidden_pre = jnp.dot(xn_two, up_full, preferred_element_type=f32)
    gate_sig = jax.nn.sigmoid(hidden_pre)
    activated = (hidden_pre * gate_sig).astype(bf16)
    mlp_sum = lax.psum(
        jnp.dot(activated, down_full, preferred_element_type=f32).astype(jnp.bfloat16), "head"
    ).astype(jnp.float32)
    node_output = (middle + mlp_sum).astype(bf16)
    down_grad = jnp.einsum("nf,nd->fd", activated, cotangent, preferred_element_type=f32)
    act_grad = jnp.einsum("nd,fd->nf", cotangent, down_full, preferred_element_type=f32)
    pre_grad = (act_grad * gate_sig * (1.0 + hidden_pre * (1.0 - gate_sig))).astype(bf16)
    up_grad = jnp.einsum("nw,nf->wf", xn_two, pre_grad, preferred_element_type=f32)
    normed_two_grad = lax.psum(
        jnp.einsum("nf,wf->nw", pre_grad, up_full, preferred_element_type=f32).astype(jnp.bfloat16),
        "head",
    ).astype(jnp.float32)
    middle_grad = cotangent.astype(f32) + norm_back(
        normed_two_grad * (1.0 + scale_two), normed_two, inverse_two
    )
    branch_grad = middle_grad.astype(bf16)
    out_grad = jnp.einsum("nh,nd->hd", heads_out, branch_grad, preferred_element_type=f32)
    mixed_grad = jnp.einsum("nd,hd->nh", branch_grad, out_full, preferred_element_type=f32).astype(
        bf16
    )
    mixed_grad_f = mixed_grad.astype(f32)
    self_dprob = jnp.sum(mixed_grad_f * values_f, axis=1)
    near_dprob = jnp.einsum("nd,nkd->nk", mixed_grad, near_values, preferred_element_type=f32)
    row_delta = self_prob * self_dprob + jnp.sum(near_prob * near_dprob, axis=1)
    self_dscore = self_prob * (self_dprob - row_delta)
    near_dscore = near_prob * (near_dprob - row_delta[:, None])
    query_grad = score_scale * (
        self_dscore[:, None] * keys_f + jnp.einsum("nk,nkd->nd", near_dscore, near_keys.astype(f32))
    )
    self_terms = jnp.concatenate(
        [score_scale * self_dscore[:, None] * queries_f, self_prob[:, None] * mixed_grad_f], axis=1
    )
    pair_terms = jnp.concatenate(
        [
            score_scale * near_dscore[:, :, None] * queries_f[:, None, :],
            near_prob[:, :, None] * mixed_grad_f[:, None, :],
        ],
        axis=2,
    )
    dense_sums = (
        jnp.zeros((table_rows.shape[0], 2 * head_dim), f32)
        .at[slot_index.reshape(-1)]
        .add(pair_terms.reshape(-1, 2 * head_dim))
    )
    remote_terms = dense_sums[2 * node_rows : 3 * node_rows]
    for offset in offsets:
        piece_rows = dense_sums[(offset + 2) * node_rows : (offset + 3) * node_rows]
        remote_terms = remote_terms + passed_along(
            piece_rows.astype(jnp.bfloat16), "node", offset
        ).astype(piece_rows.dtype)
    key_value_grad = remote_terms + self_terms
    projected_grad = jnp.concatenate([query_grad, key_value_grad], axis=1).astype(bf16)
    qkv_grad = jnp.einsum("nw,nc->wc", xn_one, projected_grad, preferred_element_type=f32)
    normed_one_grad = lax.psum(
        jnp.einsum("nc,wc->nw", projected_grad, qkv_full, preferred_element_type=f32).astype(
            jnp.bfloat16
        ),
        "head",
    ).astype(jnp.float32)
    input_grad = middle_grad + norm_back(
        normed_one_grad * (1.0 + scale_one), normed_one, inverse_one
    )
    rows_grad = jnp.concatenate(
        [
            normed_one_grad * normed_one,
            normed_one_grad,
            normed_two_grad * normed_two,
            normed_two_grad,
        ],
        axis=1,
    )
    batch_grad = jnp.dot(onehot.T, rows_grad, precision=highest)
    ada_grad = jnp.dot(sigma_embed.astype(f32).T, batch_grad, precision=highest)
    ada_sum, qkv_sum, out_sum, up_sum, down_sum = (
        lax.psum_scatter(ada_grad, "node", scatter_dimension=0, tiled=True),
        lax.psum_scatter(qkv_grad, "node", scatter_dimension=0, tiled=True),
        lax.psum_scatter(out_grad, "node", scatter_dimension=0, tiled=True),
        lax.psum_scatter(up_grad, "node", scatter_dimension=0, tiled=True),
        lax.psum_scatter(down_grad, "node", scatter_dimension=0, tiled=True),
    )
    count_value = step_count[0].astype(f32)
    ada_res = adamw_update(
        ada_master, ada_first, ada_second, ada_sum, (4 * COND) ** (-0.5), count_value
    )
    qkv_res = adamw_update(
        qkv_master, qkv_first, qkv_second, qkv_sum, (WIDTH // 2) ** (-0.5), count_value
    )
    out_res = adamw_update(
        out_master, out_first, out_second, out_sum, (WIDTH // 4) ** (-0.5), count_value
    )
    up_res = adamw_update(up_master, up_first, up_second, up_sum, WIDTH ** (-0.5), count_value)
    down_res = adamw_update(
        down_master, down_first, down_second, down_sum, HIDDEN_SIZE ** (-0.5), count_value
    )
    return (
        node_output,
        input_grad,
        ada_res[0],
        ada_res[1],
        ada_res[2],
        qkv_res[0],
        qkv_res[1],
        qkv_res[2],
        out_res[0],
        out_res[1],
        out_res[2],
        up_res[0],
        up_res[1],
        up_res[2],
        down_res[0],
        down_res[1],
        down_res[2],
    )


def solution(mesh):
    placed = (
        P("node", None),
        P("node", None),
        P(),
        P("node", None),
        P("node", None),
        P(),
        P(),
        P("node", None),
        P("node", None),
        P("node", None),
        P("node", "head"),
        P("node", "head"),
        P("node", "head"),
        P(("head", "node"), None),
        P(("head", "node"), None),
        P(("head", "node"), None),
        P("node", "head"),
        P("node", "head"),
        P("node", "head"),
        P(("head", "node"), None),
        P(("head", "node"), None),
        P(("head", "node"), None),
    )
    return jax.shard_map(
        per_device,
        mesh=mesh,
        in_specs=placed,
        out_specs=(
            P("node", None),
            P("node", None),
            P("node", None),
            P("node", None),
            P("node", None),
            P("node", "head"),
            P("node", "head"),
            P("node", "head"),
            P(("head", "node"), None),
            P(("head", "node"), None),
            P(("head", "node"), None),
            P("node", "head"),
            P("node", "head"),
            P("node", "head"),
            P(("head", "node"), None),
            P(("head", "node"), None),
            P(("head", "node"), None),
        ),
        check_vma=False,
    )
```

profile of v0, /device:TPU:0, one launch (start us, length us, event | category | flops | bytes accessed | tf_op | source)
XLA Modules:
  0.0 791.7 jit_solution(3435580741927791577)
XLA Ops:
  12.2 11.0 %all_gather.16 = bf16[512,384]{1,0:T(8,128)(2,1)S(1)} all-gather(bf16[64,384]{1,0:T(8,128)(2,1)S(1)} %convert_element_type.117), channel_id=1, replica_groups=mesh['head'=4,'node'=8] {'node'}, dimensions={0}, use_global_device_ids=true | all-gather | bytes 442368 | tf_op jit(solution)/shard_map/all_gather | solution.py:79
  24.1 16.9 %all-gather.2.cloned.1.call-done = bf16[512,2048]{1,0:T(8,128)(2,1)} async-done(((bf16[64,2048]{1,0:T(8,128)(2,1)}), bf16[512,2048]{1,0:T(8,128)(2,1)}) %all-gather.2.cloned.1.call-update) | async-done | bytes 2097168 | tf_op jit(solution)/shard_map/all_gather | solution.py:78
  43.0 5.8 fusion.47
  48.8 2.8 fusion.20
  53.9 22.5 %all_gather.17 = bf16[128,512]{1,0:T(8,128)(2,1)} all-gather(bf16[16,512]{1,0:T(8,128)(2,1)S(1)} %convert_element_type.123), channel_id=1, replica_groups=mesh['head'=4,'node'=8] {'node'}, dimensions={0}, use_global_device_ids=true | all-gather | bytes 147456 | tf_op jit(solution)/shard_map/all_gather | solution.py:80
  84.0 5.8 collective-permute-done.2
  91.8 4.8 collective-permute-done.3
  97.5 3.0 copy.96
  100.4 64.9 %gather_fusion = bf16[16384,256]{1,0:T(8,128)(2,1)} fusion(bf16[5120,256]{1,0:T(8,128)(2,1)S(1)} %copy.96, s32[16384]{0:T(1024)S(1)} %broadcast_clamp_fusion), kind=kCustom, calls=%fused_computation | custom fusion | bytes 16842752 | tf_op jit(solution)/shard_map/gather | solution.py:109
  165.3 4.6 multiply_reduce_fusion.3
  171.1 6.9 multiply_reduce_fusion.2
  180.4 11.6 %all_gather.18 = bf16[512,512]{1,0:T(8,128)(2,1)} all-gather(bf16[64,512]{1,0:T(8,128)(2,1)S(1)} %convert_element_type.127), channel_id=1, replica_groups=mesh['head'=4,'node'=8] {'node'}, dimensions={0}, use_global_device_ids=true | all-gather | bytes 589824 | tf_op jit(solution)/shard_map/all_gather | solution.py:81
  192.1 41.2 %all-reduce.5.cloned.1.call-done = bf16[1024,512]{1,0:T(8,128)(2,1)} async-done(((bf16[1024,512]{1,0:T(8,128)(2,1)}), bf16[1024,512]{1,0:T(8,128)(2,1)}) %all-reduce.5.cloned.1.call-update) | async-done | bytes 1048592 | tf_op jit(solution)/shard_map/psum | solution.py:130
  235.6 2.9 fusion.26
  238.6 2.2 multiply_convert_fusion.1
  248.0 30.9 %reduce-scatter.14.cloned.1.call-done = f32[64,512]{1,0:T(8,128)} async-done(((f32[512,512]{1,0:T(8,128)}), f32[64,512]{1,0:T(8,128)}) %reduce-scatter.14.cloned.1.call-update) | async-done | bytes 131088 | tf_op jit(solution)/shard_map/reduce_scatter | solution.py:217
  280.9 9.8 %all_gather.19 = bf16[512,512]{1,0:T(8,128)(2,1)S(1)} all-gather(bf16[64,512]{1,0:T(8,128)(2,1)S(1)} %get-tuple-element.125), channel_id=1, replica_groups=mesh['head'=4,'node'=8] {'node'}, dimensions={0}, use_global_device_ids=true | all-gather | bytes 589824 | tf_op jit(solution)/shard_map/all_gather | solution.py:82
  290.7 3.3 multiply_convert_fusion
  299.3 3.1 convolution_convert_fusion.3
  302.4 46.4 %all-reduce.7.cloned.1.call-done = bf16[1024,512]{1,0:T(8,128)(2,1)} async-done(((bf16[1024,512]{1,0:T(8,128)(2,1)}), bf16[1024,512]{1,0:T(8,128)(2,1)}) %all-reduce.7.cloned.1.call-update) | async-done | bytes 1048592 | tf_op jit(solution)/shard_map/psum | solution.py:147
  348.8 3.0 fusion.49
  351.8 3.9 convert_multiply_fusion
  355.7 3.6 broadcast_multiply_fusion.1
  361.4 5.4 multiply_reduce_fusion.1
  374.9 4.6 bitcast_multiply_fusion.1
  379.5 4.6 bitcast_multiply_fusion
  384.1 91.9 %scatter_custom_fusion = f32[5120,256]{1,0:T(8,128)} fusion(s32[16384]{0:T(1024)} %bitcast.46, f32[16384,128]{1,0:T(8,128)} %bitcast_multiply_fusion, f32[]{:T(128)} %constant.35.clone.1, f32[16384,128]{1,0:T(8,128)} %bitcast_multiply_fusion.1, f32[]{:T(128)} %constant.22.clone.1), kind=kCustom, calls=%fused_computation.2 | custom fusion | flops 8388608 | bytes 22021120 | tf_op jit(solution)/shard_map/scatter-add | solution.py:181
  476.0 6.0 copy.102
  482.0 2.8 convert.13
  486.3 2.4 collective-permute-start.4
  488.7 2.9 collective-permute-start.5
  491.6 7.7 multiply_reduce_fusion
  502.5 11.0 %collective-permute-done.7 = bf16[1024,256]{0,1:T(8,128)(2,1)} collective-permute-done((bf16[1024,256]{0,1:T(8,128)(2,1)}, bf16[1024,256]{0,1:T(8,128)(2,1)}, u32[]{:S(2)}, u32[]{:S(2)}) %collective-permute-start.7) | collective-permute-done | bytes 524320 | tf_op jit(solution)/shard_map/ppermute | solution.py:21
  513.6 9.2 %collective-permute-done.6 = bf16[1024,256]{0,1:T(8,128)(2,1)} collective-permute-done((bf16[1024,256]{0,1:T(8,128)(2,1)}, bf16[1024,256]{0,1:T(8,128)(2,1)}, u32[]{:S(2)}, u32[]{:S(2)}) %collective-permute-start.6) | collective-permute-done | bytes 524320 | tf_op jit(solution)/shard_map/ppermute | solution.py:21
  522.8 2.4 fusion.35
  527.8 2.6 fusion.44
  530.5 3.3 fusion.73
  537.4 76.4 %all-reduce.9.cloned.1.call-done = (bf16[1024,512]{1,0:T(8,128)(2,1)}, bf16[1024,512]{1,0:T(8,128)(2,1)}) async-done(((bf16[1024,512]{1,0:T(8,128)(2,1)}, bf16[1024,512]{1,0:T(8,128)(2,1)}), (bf16[1024,512]{1,0:T(8,128)(2,1)}, bf16[1024,512]{1,0:T(8,128)(2,1)})) %all-reduce.9.cloned.1.call-update) | async-done | bytes 2097168 | tf_op jit(solution)/shard_map/psum | solution.py:139
  615.4 3.5 fusion.50
  618.9 2.9 fusion.4
  621.8 3.8 convolution_bitcast_fusion
  625.6 5.5 copy.124
  631.1 18.9 %reduce-scatter.10.cloned.1.call-done = f32[16,512]{1,0:T(8,128)} async-done(((f32[128,512]{1,0:T(8,128)}), f32[16,512]{1,0:T(8,128)}) %reduce-scatter.10.cloned.1.call-update) | async-done | bytes 32784 | tf_op jit(solution)/shard_map/reduce_scatter | solution.py:215
  651.4 37.7 %reduce-scatter.12.cloned.1.call-done = f32[64,512]{1,0:T(8,128)} async-done(((f32[512,512]{1,0:T(8,128)}), f32[64,512]{1,0:T(8,128)}) %reduce-scatter.12.cloned.1.call-update) | async-done | bytes 131088 | tf_op jit(solution)/shard_map/reduce_scatter | solution.py:216
  690.9 36.4 %reduce-scatter.8.cloned.1.call-done = f32[64,384]{1,0:T(8,128)} async-done(((f32[512,384]{1,0:T(8,128)}), f32[64,384]{1,0:T(8,128)}) %reduce-scatter.8.cloned.1.call-update) | async-done | bytes 98320 | tf_op jit(solution)/shard_map/reduce_scatter | solution.py:214
  729.7 4.2 fusion.24
  733.9 47.9 %reduce-scatter.16.cloned.1.call-done = f32[64,2048]{1,0:T(8,128)} async-done(((f32[512,2048]{1,0:T(8,128)}), f32[64,2048]{1,0:T(8,128)}) %reduce-scatter.16.cloned.1.call-update) | async-done | bytes 524304 | tf_op jit(solution)/shard_map/reduce_scatter | solution.py:213
  781.8 2.9 multiply_subtract_fusion
  (205 shorter events, 68.3 us)
Async XLA Ops:
  7.2 33.8 %copy-start = (bf16[4,512]{1,0:T(4,128)(2,1)S(1)}, bf16[4,512]{1,0:T(4,128)(2,1)}, u32[]{:S(2)}) copy-start(bf16[4,512]{1,0:T(4,128)(2,1)} %param.24) | copy-start | bytes 12292
  7.2 4.8 copy-start.51
  7.2 16.1 %copy-start.1 = (bf16[1024,512]{1,0:T(8,128)(2,1)S(1)}, bf16[1024,512]{1,0:T(8,128)(2,1)}, u32[]{:S(2)}) copy-start(bf16[1024,512]{1,0:T(8,128)(2,1)} %param.22) | copy-start | bytes 3145732
  7.2 33.8 %all-gather.2.cloned.1.call-start = ((), (), s32[]{:S(2)}) async-start(), calls=%async_computation.5 | async-start | bytes 2359296 | tf_op jit(solution)/shard_map/all_gather | solution.py:78
  9.2 224.2 %all-reduce.5.cloned.1.call-start = ((), (), s32[]{:S(2)}) async-start(), calls=%async_computation.6 | async-start | bytes 2097152 | tf_op jit(solution)/shard_map/psum | solution.py:130
  23.2 28.4 %copy-start.32 = (bf16[512,384]{1,0:T(8,128)(2,1)}, bf16[512,384]{1,0:T(8,128)(2,1)S(1)}, u32[]{:S(2)}) copy-start(bf16[512,384]{1,0:T(8,128)(2,1)S(1)} %all_gather.16) | copy-start | bytes 1179652
  24.1 24.7 %copy-start.43 = (f32[1024]{0:T(1024)}, f32[1024]{0:T(1024)S(1)}, u32[]{:S(2)}) copy-start(f32[1024]{0:T(1024)S(1)} %add_rsqrt_fusion.1) | copy-start | bytes 12292
  51.6 26.1 %copy-start.21 = (bf16[1024,512]{1,0:T(8,128)(2,1)}, bf16[1024,512]{1,0:T(8,128)(2,1)S(1)}, u32[]{:S(2)}) copy-start(bf16[1024,512]{1,0:T(8,128)(2,1)S(1)} %fusion.20) | copy-start | bytes 3145732
  52.3 28.1 %collective-permute-start = (bf16[1024,256]{0,1:T(8,128)(2,1)S(1)}, bf16[1024,256]{0,1:T(8,128)(2,1)S(1)}, u32[]{:S(2)}, u32[]{:S(2)}) collective-permute-start(bf16[1024,256]{0,1:T(8,128)(2,1)S(1)} %slice.77), channel_id=1, source_target_pairs={{6,0},{7,1},{0,2},{1,3},{2,4},{3,5},{4,6},{5,7},{14,8},{15,9},{8,1... | collective-permute-start | bytes 1572872 | tf_op jit(solution)/shard_map/ppermute | solution.py:21
  53.9 27.4 %collective-permute-start.1 = (bf16[1024,256]{0,1:T(8,128)(2,1)S(1)}, bf16[1024,256]{0,1:T(8,128)(2,1)}, u32[]{:S(2)}, u32[]{:S(2)}) collective-permute-start(bf16[1024,256]{0,1:T(8,128)(2,1)S(1)} %slice.77), channel_id=1, source_target_pairs={{7,0},{0,1},{1,2},{2,3},{3,4},{4,5},{5,6},{6,7},{15,8},{8,9},{9,10... | collective-permute-start | bytes 1572872 | tf_op jit(solution)/shard_map/ppermute | solution.py:21
  76.4 13.4 %collective-permute-start.2 = (bf16[1024,256]{0,1:T(8,128)(2,1)S(1)}, bf16[1024,256]{0,1:T(8,128)(2,1)}, u32[]{:S(2)}, u32[]{:S(2)}) collective-permute-start(bf16[1024,256]{0,1:T(8,128)(2,1)S(1)} %slice.77), channel_id=1, source_target_pairs={{1,0},{2,1},{3,2},{4,3},{5,4},{6,5},{7,6},{0,7},{9,8},{10,9},{11,1... | collective-permute-start | bytes 1572872 | tf_op jit(solution)/shard_map/ppermute | solution.py:21
  77.8 18.8 %collective-permute-start.3 = (bf16[1024,256]{0,1:T(8,128)(2,1)S(1)}, bf16[1024,256]{0,1:T(8,128)(2,1)S(1)}, u32[]{:S(2)}, u32[]{:S(2)}) collective-permute-start(bf16[1024,256]{0,1:T(8,128)(2,1)S(1)} %slice.77), channel_id=1, source_target_pairs={{2,0},{3,1},{4,2},{5,3},{6,4},{7,5},{0,6},{1,7},{10,8},{11,9},{12,... | collective-permute-start | bytes 1572872 | tf_op jit(solution)/shard_map/ppermute | solution.py:21
  165.3 4.8 copy-start.24
  170.2 8.0 %copy-start.45 = (f32[1024]{0:T(1024)}, f32[1024]{0:T(1024)S(1)}, u32[]{:S(2)}) copy-start(f32[1024]{0:T(1024)S(1)} %get-tuple-element.127) | copy-start | bytes 12292
  178.2 55.1 %copy-start.2 = (bf16[1024,512]{1,0:T(8,128)(2,1)S(1)}, bf16[1024,512]{1,0:T(8,128)(2,1)}, u32[]{:S(2)}) copy-start(bf16[1024,512]{1,0:T(8,128)(2,1)} %param.22) | copy-start | bytes 3145732
  178.9 13.2 %copy-start.10 = (bf16[1024,128]{0,1:T(8,128)(2,1)}, bf16[1024,128]{0,1:T(8,128)(2,1)S(1)}, u32[]{:S(2)}) copy-start(bf16[1024,128]{0,1:T(8,128)(2,1)S(1)} %fusion.41) | copy-start | bytes 786436
  180.4 98.6 %reduce-scatter.14.cloned.1.call-start = ((), (), s32[]{:S(2)}) async-start(), calls=%async_computation.11 | async-start | bytes 1179648 | tf_op jit(solution)/shard_map/reduce_scatter | solution.py:217
  243.5 105.2 %all-reduce.7.cloned.1.call-start = ((), (), s32[]{:S(2)}) async-start(), calls=%async_computation.7 | async-start | bytes 2097152 | tf_op jit(solution)/shard_map/psum | solution.py:147
  290.7 4.3 copy-start.30
  296.7 317.1 %all-reduce.9.cloned.1.call-start = ((), (), s32[]{:S(2)}) async-start(), calls=%async_computation.13 | async-start | bytes 4194304 | tf_op jit(solution)/shard_map/psum | solution.py:139
  299.3 49.4 %copy-start.42 = (f32[1024]{0:T(1024)S(1)}, f32[1024]{0:T(1024)}, u32[]{:S(2)}) copy-start(f32[1024]{0:T(1024)} %copy-done.41) | copy-start | bytes 12292
  351.8 3.9 copy-start.46
  361.4 6.7 copy-start.20
  361.4 6.7 copy-start.47
  366.8 8.2 %copy-start.7 = (f32[1024,128]{1,0:T(8,128)S(1)}, f32[1024,128]{1,0:T(8,128)}, u32[]{:S(2)}) copy-start(f32[1024,128]{1,0:T(8,128)} %copy.128) | copy-start | bytes 1572868
  374.9 4.6 copy-start.9
  374.9 4.6 copy-start.35
  484.9 6.7 copy-start.14
  486.3 16.2 %collective-permute-start.4 = (bf16[1024,256]{0,1:T(8,128)(2,1)}, bf16[1024,256]{0,1:T(8,128)(2,1)}, u32[]{:S(2)}, u32[]{:S(2)}) collective-permute-start(bf16[1024,256]{0,1:T(8,128)(2,1)} %get-tuple-element.114), channel_id=1, source_target_pairs={{2,0},{3,1},{4,2},{5,3},{6,4},{7,5},{0,6},{1,7},{10,8},{11,9},{12,... | collective-permute-start | bytes 1572872 | tf_op jit(solution)/shard_map/ppermute | solution.py:21
  488.7 24.9 %collective-permute-start.7 = (bf16[1024,256]{0,1:T(8,128)(2,1)}, bf16[1024,256]{0,1:T(8,128)(2,1)}, u32[]{:S(2)}, u32[]{:S(2)}) collective-permute-start(bf16[1024,256]{0,1:T(8,128)(2,1)} %get-tuple-element.115), channel_id=1, source_target_pairs={{6,0},{7,1},{0,2},{1,3},{2,4},{3,5},{4,6},{5,7},{14,8},{15,9},{8,1... | collective-permute-start | bytes 1572872 | tf_op jit(solution)/shard_map/ppermute | solution.py:21
  488.7 34.0 %collective-permute-start.6 = (bf16[1024,256]{0,1:T(8,128)(2,1)}, bf16[1024,256]{0,1:T(8,128)(2,1)}, u32[]{:S(2)}, u32[]{:S(2)}) collective-permute-start(bf16[1024,256]{0,1:T(8,128)(2,1)} %get-tuple-element.116), channel_id=1, source_target_pairs={{7,0},{0,1},{1,2},{2,3},{3,4},{4,5},{5,6},{6,7},{15,8},{8,9},{9,10... | collective-permute-start | bytes 1572872 | tf_op jit(solution)/shard_map/ppermute | solution.py:21
  488.7 12.6 %copy-start.49 = (f32[1024]{0:T(1024)S(1)}, f32[1024]{0:T(1024)}, u32[]{:S(2)}) copy-start(f32[1024]{0:T(1024)} %get-tuple-element.106) | copy-start | bytes 12292
  488.7 12.6 %copy-start.50 = (f32[1024]{0:T(1024)S(1)}, f32[1024]{0:T(1024)}, u32[]{:S(2)}) copy-start(f32[1024]{0:T(1024)} %get-tuple-element.107) | copy-start | bytes 12292
  488.7 34.0 %collective-permute-start.5 = (bf16[1024,256]{0,1:T(8,128)(2,1)}, bf16[1024,256]{0,1:T(8,128)(2,1)}, u32[]{:S(2)}, u32[]{:S(2)}) collective-permute-start(bf16[1024,256]{0,1:T(8,128)(2,1)} %get-tuple-element.117), channel_id=1, source_target_pairs={{1,0},{2,1},{3,2},{4,3},{5,4},{6,5},{7,6},{0,7},{9,8},{10,9},{11,1... | collective-permute-start | bytes 1572872 | tf_op jit(solution)/shard_map/ppermute | solution.py:21
  499.2 23.5 %copy-start.13 = (f32[1024,128]{0,1:T(8,128)S(1)}, f32[1024,128]{0,1:T(8,128)}, u32[]{:S(2)}) copy-start(f32[1024,128]{0,1:T(8,128)} %get-tuple-element.123) | copy-start | bytes 1572868
  502.5 22.7 %copy-start.36 = (bf16[1024,128]{0,1:T(8,128)(2,1)}, bf16[1024,128]{0,1:T(8,128)(2,1)S(1)}, u32[]{:S(2)}) copy-start(bf16[1024,128]{0,1:T(8,128)(2,1)S(1)} %get-tuple-element.121) | copy-start | bytes 786436
  527.7 122.3 %reduce-scatter.10.cloned.1.call-start = ((), (), s32[]{:S(2)}) async-start(), calls=%async_computation.9 | async-start | bytes 294912 | tf_op jit(solution)/shard_map/reduce_scatter | solution.py:215
  530.4 158.7 %reduce-scatter.12.cloned.1.call-start = ((), (), s32[]{:S(2)}) async-start(), calls=%async_computation.10 | async-start | bytes 1179648 | tf_op jit(solution)/shard_map/reduce_scatter | solution.py:216
  533.8 193.4 %reduce-scatter.8.cloned.1.call-start = ((), (), s32[]{:S(2)}) async-start(), calls=%async_computation.8 | async-start | bytes 884736 | tf_op jit(solution)/shard_map/reduce_scatter | solution.py:214
  537.3 78.0 %copy-start.44 = (f32[1024]{0:T(1024)S(1)}, f32[1024]{0:T(1024)}, u32[]{:S(2)}) copy-start(f32[1024]{0:T(1024)} %copy-done.43) | copy-start | bytes 12292
  537.4 244.5 %reduce-scatter.16.cloned.1.call-start = ((), (), s32[]{:S(2)}) async-start(), calls=%async_computation.12 | async-start | bytes 4718592 | tf_op jit(solution)/shard_map/reduce_scatter | solution.py:213
  615.4 3.5 copy-start.12
  615.4 3.5 copy-start.15
  631.1 18.9 %copy-start.40 = (f32[16,512]{1,0:T(8,128)S(1)}, f32[16,512]{1,0:T(8,128)}, u32[]{:S(2)}) copy-start(f32[16,512]{1,0:T(8,128)} %param.35) | copy-start | bytes 98308
  631.1 58.1 %copy-start.28 = (f32[64,512]{1,0:T(8,128)S(1)}, f32[64,512]{1,0:T(8,128)}, u32[]{:S(2)}) copy-start(f32[64,512]{1,0:T(8,128)} %param.38) | copy-start | bytes 393220
  631.1 58.1 %copy-start.38 = (f32[64,512]{1,0:T(8,128)S(1)}, f32[64,512]{1,0:T(8,128)}, u32[]{:S(2)}) copy-start(f32[64,512]{1,0:T(8,128)} %param.40) | copy-start | bytes 393220
  631.1 96.2 %copy-start.34 = (f32[64,384]{1,0:T(8,128)S(1)}, f32[64,384]{1,0:T(8,128)}, u32[]{:S(2)}) copy-start(f32[64,384]{1,0:T(8,128)} %param.32) | copy-start | bytes 294916
  631.1 98.6 %copy-start.48 = (f32[1024]{0:T(1024)S(1)}, f32[1024]{0:T(1024)}, u32[]{:S(2)}) copy-start(f32[1024]{0:T(1024)} %get-tuple-element.86) | copy-start | bytes 12292
  (23 other events, 47.5 us)
Sparse Core Ops, SparseCore 0:
  10.5 30.4 all-gather.1
  180.5 52.7 all-reduce.4
  243.7 35.2 reduce-scatter.13
  296.8 51.8 all-reduce.6
  527.8 85.8 all-reduce.8
  617.2 32.6 reduce-scatter.9
  653.1 35.9 reduce-scatter.11
  692.3 34.9 reduce-scatter.7
  730.6 51.1 reduce-scatter.15
where the time goes:
time: 798 us; the launch traced here: 792 us
  waiting for transfers between devices  384 us (48%)
  other arithmetic  178 us (22%)
  local copies, waits for them, and re-layouts  108 us (14%)
  blocking collectives  54.9 us (7%)
  matrix products  41.5 us (5%)
  between operations  15.7 us (2%)
  starting transfers between devices  10.2 us (1%)
    scatter-add x1, other arithmetic, per_device(): dense_sums = jnp.zeros((table_rows.shape[0], 2 * head_dim), f32).at[slot_...  91.9 us
    psum x1, waiting for transfers between devices, per_device(): lax.psum(jnp.dot(activated, down_full, preferred_element_type=f32).astype...  76.4 us
    gather x1, local copies, waits for them, and re-layouts, per_device(): near_rows = table_rows[slot_index]  64.9 us
    reduce_scatter x1, waiting for transfers between devices, per_device(): lax.psum_scatter(ada_grad, 'node', scatter_dimension=0, tiled=True)  47.9 us
    psum x1, waiting for transfers between devices, per_device(): lax.psum(jnp.einsum('nf,wf->nw', pre_grad, up_full, preferred_element_typ...  46.4 us
    psum x1, waiting for transfers between devices, per_device(): lax.psum(jnp.dot(heads_out, out_full, preferred_element_type=f32).astype(...  41.2 us
    reduce_scatter x1, waiting for transfers between devices, per_device(): lax.psum_scatter(up_grad, 'node', scatter_dimension=0, tiled=True)  37.7 us
    reduce_scatter x1, waiting for transfers between devices, per_device(): lax.psum_scatter(qkv_grad, 'node', scatter_dimension=0, tiled=True)  36.4 us
  transfers between devices with their start and end apart: 17, of which 13 were waited for; matrix products, arithmetic and copies ran while one was open for 8% of the time, Pallas kernels for 0%

commit v1 on v0

--- a/solution.py
+++ b/solution.py
@@ -1,7 +1,13 @@
+import functools
+import math
+
 import jax
 import jax.numpy as jnp
 from jax import lax
+from jax.experimental import pallas as pl
+from jax.experimental.pallas import tpu as pltpu
 from jax.sharding import PartitionSpec as P
+
 
 WIDTH = 512
 HIDDEN_SIZE = 2048
@@ -40,6 +46,139 @@
     normed_step = first_new / correct / (jnp.sqrt(second_new / correct) + adam_eps)
     master_new = master - rate * (normed_step + weight_decay * master)
     return (master_new, first_new, second_new)
+
+
+f32=jnp.float32; bf16=jnp.bfloat16
+NT=(((1,),(1,)),((),()))
+SPAN=256
+
+def count_groups(cnt, hik, lok, rows):
+    steps=hik.shape[0]
+    parts=rows//SPAN
+    total=5*parts*16
+    rowid=lax.broadcasted_iota(jnp.int32,(total,1),0)
+    rowkey=lax.div(rowid,16)*16+lax.rem(rowid,16)
+    spot=lax.broadcasted_iota(jnp.int32,(SPAN,1),0)
+    def body(g,_):
+        keys=hik[pl.ds(g,1),:]
+        low=lok[pl.ds(g,1),:]
+        left=jnp.where(rowkey==keys,1.0,0.0).astype(bf16)
+        right=jnp.where(spot==low,1.0,0.0).astype(bf16)
+        made=lax.dot_general(left,right,NT,preferred_element_type=f32).astype(bf16)
+        at=pl.multiple_of(g*16,16)
+        for b in range(5):
+            for p in range(parts):
+                r=(b*parts+p)*16
+                cnt[b,pl.ds(at,16),p*SPAN:(p+1)*SPAN]=made[r:r+16,:]
+        return 0
+    lax.fori_loop(0,steps,body,0)
+
+def add_self(cnt, block, rows):
+    eye=(lax.broadcasted_iota(jnp.int32,(SPAN,SPAN),0)==lax.broadcasted_iota(jnp.int32,(SPAN,SPAN),1))
+    one=jnp.where(eye,1.0,0.0).astype(bf16)
+    for p in range(rows//SPAN):
+        s=slice(p*SPAN,(p+1)*SPAN)
+        cnt[block,s,s]=cnt[block,s,s]+one
+
+def attend_block(b, first, q, keys, vals, cnt, e, m, l, acc, fac, chunk, scale):
+    rows=q.shape[0]
+    lane=lax.broadcasted_iota(jnp.int32,(chunk,128),1)
+    def body(i,_):
+        at=pl.ds(pl.multiple_of(i*chunk,chunk),chunk)
+        s=lax.dot_general(q[at,:],keys,NT,preferred_element_type=f32)*scale
+        c=cnt[b,at,:].astype(f32)
+        s=jnp.where(c>0,s,-1e30)
+        top=jnp.max(s,axis=1,keepdims=True)
+        if not first:
+            old=m[at,0:1]
+            top=jnp.maximum(top,old)
+        w=(jnp.exp2(s-top)*c)
+        total=jnp.sum(w,axis=1,keepdims=True)
+        w=w.astype(bf16)
+        e[b,at,:]=w
+        out=jnp.dot(w,vals,preferred_element_type=f32)
+        if first:
+            acc[at,:]=out; l[at,:]=jnp.broadcast_to(total,(chunk,128))
+            fac[at,:]=jnp.where(lane==b,top,0.0)
+        else:
+            shrink=jnp.exp2(old-top)
+            acc[at,:]=acc[at,:]*shrink+out
+            l[at,:]=l[at,:]*shrink+total
+            fac[at,:]=jnp.where(lane==b,top,fac[at,:])
+        m[at,:]=jnp.broadcast_to(top,(chunk,128))
+        return 0
+    lax.fori_loop(0,rows//chunk,body,0)
+
+def fwd_kernel(order, self_block, scale, q, kv, hik, lok, att, e, fac, cnt, m, l):
+    rows=q.shape[0]
+    count_groups(cnt,hik,lok,rows)
+    add_self(cnt,self_block,rows)
+    for t,b in enumerate(order):
+        attend_block(b,t==0,q,kv[b,:,:128],kv[b,:,128:],cnt,e,m,l,att,fac,256,scale)
+    inv=1.0/l[...]
+    att[...]=att[...]*inv
+    fac[...]=jnp.exp2(fac[...]-m[...])*inv
+
+def attention_fwd(q,kv,hik,lok,scale):
+    rows=q.shape[0]
+    V=pltpu.VMEM
+    full=pl.BlockSpec(memory_space=V)
+    return pl.pallas_call(functools.partial(fwd_kernel,(2,1,3,0,4),2,scale*math.log2(math.e)),
+        out_shape=(jax.ShapeDtypeStruct((rows,128),f32),jax.ShapeDtypeStruct((5,rows,rows),bf16),jax.ShapeDtypeStruct((rows,128),f32)),
+        in_specs=[full]*4,out_specs=(full,)*3,
+        scratch_shapes=[V((5,rows,rows),bf16),V((rows,128),f32),V((rows,128),f32)],
+        compiler_params=pltpu.CompilerParams(vmem_limit_bytes=60<<20),name="attend_fwd")(q,kv,hik,lok)
+
+def back_block(b, q_t, do, fac, delta, kv, e, dq, dkv, first, chunk, keyscale):
+    rows=do.shape[0]
+    f=fac[:,b:b+1]
+    dob=(do*f)
+    dobh=dob.astype(bf16)
+    d=-(delta*f)
+    h=d.astype(bf16); r=d-h.astype(f32); h2=r.astype(bf16); h3=(r-h2.astype(f32)).astype(bf16)
+    lane=lax.broadcasted_iota(jnp.int32,(rows,128),1)
+    zero=jnp.zeros((rows,128),bf16)
+    dcol=jnp.where(lane==0,h.astype(f32),jnp.where(lane==1,h2.astype(f32),jnp.where(lane==2,h3.astype(f32),0.0))).astype(bf16)
+    left=jnp.concatenate([dobh,dcol],axis=1)
+    dob_t=dobh.T
+    ones=jnp.ones((chunk,128),bf16)
+    for i in range(kv.shape[1]//chunk):
+        s=slice(i*chunk,(i+1)*chunk)
+        right=jnp.concatenate([kv[b,s,128:],ones],axis=1)
+        dp=lax.dot_general(left,right,NT,preferred_element_type=f32)
+        w=e[b,:,s]
+        ds=(dp*w.astype(f32)).astype(bf16)
+        dkv[b,:128,s]=jnp.dot(q_t,ds,preferred_element_type=f32)*keyscale
+        dkv[b,128:,s]=jnp.dot(dob_t,w,preferred_element_type=f32)
+        out=jnp.dot(ds,kv[b,s,:128],preferred_element_type=f32)
+        if first and i==0: dq[...]=out
+        else: dq[...]+=out
+
+def bwd_kernel(scale, q, do, att, fac, kv, e, dq, dkv, ):
+    q_t=q[...].T
+    dof=do[...].astype(f32)
+    delta=jnp.sum(dof*att[...],axis=1,keepdims=True)
+    for t,b in enumerate((0,4,1,3,2)):
+        back_block(b,q_t,dof,fac,delta,kv,e,dq,dkv,t==0,512,scale)
+    dq[...]=dq[...]*scale
+
+def attention_bwd(q,do,att,fac,kv,e,scale):
+    rows=q.shape[0]
+    V=pltpu.VMEM
+    full=pl.BlockSpec(memory_space=V)
+    return pl.pallas_call(functools.partial(bwd_kernel,scale),
+        out_shape=(jax.ShapeDtypeStruct((rows,128),f32),jax.ShapeDtypeStruct((5,256,rows),f32)),
+        in_specs=[full]*6,out_specs=(full,)*2,
+        compiler_params=pltpu.CompilerParams(vmem_limit_bytes=60<<20),name="attend_bwd")(q,do,att,fac,kv,e)
+
+def tables(slot_index, valid, rows):
+    parts=rows//SPAN
+    flat=slot_index.reshape(-1,256)
+    ok=(valid>0).reshape(-1,256)
+    node=lax.broadcasted_iota(jnp.int32,flat.shape,1)//16
+    hi=jnp.where(ok,(flat//SPAN)*16+node,-1)
+    lo=flat%SPAN
+    return hi,lo
 
 
 def per_device(
@@ -74,20 +213,23 @@
     score_scale = head_dim ** (-0.5)
     node_index = lax.axis_index("node")
     total_nodes = node_rows * lax.axis_size("node")
-    ada_full, qkv_full, out_full, up_full, down_full = (
-        lax.all_gather(ada_master.astype(bf16), "node", axis=0, tiled=True),
+    qkv_full, out_full, up_full, down_full = (
         lax.all_gather(qkv_master.astype(bf16), "node", axis=0, tiled=True),
         lax.all_gather(out_master.astype(bf16), "node", axis=0, tiled=True),
         lax.all_gather(up_master.astype(bf16), "node", axis=0, tiled=True),
         lax.all_gather(down_master.astype(bf16), "node", axis=0, tiled=True),
     )
+    cond_rows = ada_master.shape[0]
+    sigma_part = lax.dynamic_slice_in_dim(sigma_embed, node_index * cond_rows, cond_rows, 1)
     limits = jnp.cumsum(batch_counts)[:-1]
     positions = node_index * node_rows + jnp.arange(node_rows, dtype=jnp.int32)
     member = jnp.sum((positions[:, None] >= limits[None, :]).astype(jnp.int32), axis=1)
     onehot = (
         member[:, None] == jnp.arange(batch_counts.shape[0], dtype=jnp.int32)[None, :]
     ).astype(f32)
-    modulation = jnp.dot(sigma_embed, ada_full, preferred_element_type=f32)
+    modulation = lax.psum(
+        jnp.dot(sigma_part, ada_master.astype(bf16), preferred_element_type=f32), "node"
+    )
     per_node = jnp.dot(onehot, modulation, precision=highest)
     scale_one = per_node[:, :model_width]
     shift_one = per_node[:, model_width : 2 * model_width]
@@ -98,34 +240,14 @@
     projected = jnp.dot(xn_one, qkv_full, preferred_element_type=f32).astype(bf16)
     queries = projected[:, :head_dim]
     keys_values = projected[:, head_dim:]
-    key_rows = keys_values[:, :head_dim]
-    value_rows = keys_values[:, head_dim:]
     offsets = (-2, -1, 1, 2)
     fetched = {0: keys_values}
     for offset in offsets:
         fetched[offset] = passed_along(keys_values, "node", -offset)
-    table_rows = jnp.concatenate([fetched[offset] for offset in (-2, -1, 0, 1, 2)], axis=0)
+    table = jnp.stack([fetched[offset] for offset in (-2, -1, 0, 1, 2)], axis=0)
     slot_index = jnp.mod(neighbours - (node_index - 2) * node_rows, total_nodes)
-    near_rows = table_rows[slot_index]
-    near_keys = near_rows[:, :, :head_dim]
-    near_values = near_rows[:, :, head_dim:]
-    is_valid = neighbour_valid > 0
-    queries_f = queries.astype(f32)
-    keys_f = key_rows.astype(f32)
-    values_f = value_rows.astype(f32)
-    near_values_f = near_values.astype(f32)
-    self_score = jnp.sum(queries_f * keys_f, axis=1) * score_scale
-    near_score = (
-        jnp.einsum("nd,nkd->nk", queries, near_keys, preferred_element_type=f32) * score_scale
-    )
-    near_score = jnp.where(is_valid, near_score, -1e30)
-    row_max = jnp.maximum(jnp.max(near_score, axis=1), self_score)
-    self_exp = jnp.exp(self_score - row_max)
-    near_exp = jnp.exp(near_score - row_max[:, None])
-    denominator = self_exp + jnp.sum(near_exp, axis=1)
-    self_prob = self_exp / denominator
-    near_prob = near_exp / denominator[:, None]
-    mixed = self_prob[:, None] * values_f + jnp.einsum("nk,nkd->nd", near_prob, near_values_f)
+    high_keys, low_keys = tables(slot_index, neighbour_valid, node_rows)
+    mixed, weights, factors = attention_fwd(queries, table, high_keys, low_keys, score_scale)
     heads_out = mixed.astype(bf16)
     branch = lax.psum(
         jnp.dot(heads_out, out_full, preferred_element_type=f32).astype(jnp.bfloat16), "head"
@@ -156,37 +278,15 @@
     mixed_grad = jnp.einsum("nd,hd->nh", branch_grad, out_full, preferred_element_type=f32).astype(
         bf16
     )
-    mixed_grad_f = mixed_grad.astype(f32)
-    self_dprob = jnp.sum(mixed_grad_f * values_f, axis=1)
-    near_dprob = jnp.einsum("nd,nkd->nk", mixed_grad, near_values, preferred_element_type=f32)
-    row_delta = self_prob * self_dprob + jnp.sum(near_prob * near_dprob, axis=1)
-    self_dscore = self_prob * (self_dprob - row_delta)
-    near_dscore = near_prob * (near_dprob - row_delta[:, None])
-    query_grad = score_scale * (
-        self_dscore[:, None] * keys_f + jnp.einsum("nk,nkd->nd", near_dscore, near_keys.astype(f32))
-    )
-    self_terms = jnp.concatenate(
-        [score_scale * self_dscore[:, None] * queries_f, self_prob[:, None] * mixed_grad_f], axis=1
-    )
-    pair_terms = jnp.concatenate(
-        [
-            score_scale * near_dscore[:, :, None] * queries_f[:, None, :],
-            near_prob[:, :, None] * mixed_grad_f[:, None, :],
-        ],
-        axis=2,
-    )
-    dense_sums = (
-        jnp.zeros((table_rows.shape[0], 2 * head_dim), f32)
-        .at[slot_index.reshape(-1)]
-        .add(pair_terms.reshape(-1, 2 * head_dim))
-    )
-    remote_terms = dense_sums[2 * node_rows : 3 * node_rows]
+    query_grad, pair_sums = attention_bwd(
+        queries, mixed_grad, mixed, factors, table, weights, score_scale
+    )
+    remote_terms = pair_sums[2]
     for offset in offsets:
-        piece_rows = dense_sums[(offset + 2) * node_rows : (offset + 3) * node_rows]
         remote_terms = remote_terms + passed_along(
-            piece_rows.astype(jnp.bfloat16), "node", offset
-        ).astype(piece_rows.dtype)
-    key_value_grad = remote_terms + self_terms
+            pair_sums[offset + 2].astype(bf16), "node", offset
+        ).astype(f32)
+    key_value_grad = remote_terms.T
     projected_grad = jnp.concatenate([query_grad, key_value_grad], axis=1).astype(bf16)
     qkv_grad = jnp.einsum("nw,nc->wc", xn_one, projected_grad, preferred_element_type=f32)
     normed_one_grad = lax.psum(
@@ -208,9 +308,9 @@
         axis=1,
     )
     batch_grad = jnp.dot(onehot.T, rows_grad, precision=highest)
-    ada_grad = jnp.dot(sigma_embed.astype(f32).T, batch_grad, precision=highest)
-    ada_sum, qkv_sum, out_sum, up_sum, down_sum = (
-        lax.psum_scatter(ada_grad, "node", scatter_dimension=0, tiled=True),
+    batch_grad = lax.psum(batch_grad, "node")
+    ada_sum = jnp.dot(sigma_part.astype(f32).T, batch_grad, precision=highest)
+    qkv_sum, out_sum, up_sum, down_sum = (
         lax.psum_scatter(qkv_grad, "node", scatter_dimension=0, tiled=True),
         lax.psum_scatter(out_grad, "node", scatter_dimension=0, tiled=True),
         lax.psum_scatter(up_grad, "node", scatter_dimension=0, tiled=True),

time: 798 us -> 579 us (0.73)
  other arithmetic: 178 us -> 37 us
  waiting for transfers between devices: 384 us -> 281 us
  local copies, waits for them, and re-layouts: 108 us -> 22.8 us
  blocking collectives: 54.9 us -> 113 us
  Pallas kernels: 0 us -> 56.8 us
    scatter-add x1 -> x0, other arithmetic: 91.9 us -> none  [per_device(): dense_sums = jnp.zeros((table_rows.shape[0], 2 * head_dim), f32).at[slot_...]
    gather x1 -> x0, local copies, waits for them, and re-layouts: 64.9 us -> none  [per_device(): near_rows = table_rows[slot_index]]
    pallas_call x0 -> x2, Pallas kernels: none -> 56.8 us  [the longest x1 39.9 us: attention_fwd(): pl.pallas_call(functools.partial(fwd_kernel, (2, 1, 3, 0, 4), 2, scale *...]
    psum x0 -> x2, blocking collectives: none -> 49.2 us  [the longest x1 25.5 us: per_device(): lax.psum(jnp.dot(sigma_part, ada_master.astype(bf16), preferred_element_t...]
    reduce_scatter x1 -> x0, waiting for transfers between devices: 47.9 us -> none  [per_device(): lax.psum_scatter(ada_grad, 'node', scatter_dimension=0, tiled=True)]
    reduce_scatter x1, waiting for transfers between devices: 37.7 us -> 0.01 us  [per_device(): lax.psum_scatter(up_grad, 'node', scatter_dimension=0, tiled=True)]
    unnamed x4 -> x0, other arithmetic: 24.6 us -> none
    reduce_scatter x1, waiting for transfers between devices: 18.9 us -> 0.01 us  [per_device(): lax.psum_scatter(out_grad, 'node', scatter_dimension=0, tiled=True)]
  transfers between devices with their start and end apart: 17 -> 15, of which waited for: 13 -> 8; matrix products, arithmetic and copies ran while one was open for 8% -> 6% of each run, Pallas kernels for 0% -> 3%
where the time goes in v1:
time: 579 us; the launch traced here: 572 us
  waiting for transfers between devices  281 us (49%)
  blocking collectives  113 us (20%)
  Pallas kernels  56.8 us (10%)
  other arithmetic  37 us (6%)
  matrix products  36.6 us (6%)
  local copies, waits for them, and re-layouts  22.8 us (4%)
  between operations  15.8 us (3%)
  starting transfers between devices  9.08 us (2%)
    psum x1, waiting for transfers between devices, per_device(): lax.psum(jnp.dot(activated, down_full, preferred_element_type=f32).astype...  87.4 us
    psum x1, waiting for transfers between devices, per_device(): lax.psum(jnp.einsum('nf,wf->nw', pre_grad, up_full, preferred_element_typ...  52 us
    psum x1, waiting for transfers between devices, per_device(): lax.psum(jnp.dot(heads_out, out_full, preferred_element_type=f32).astype(...  41.5 us
    pallas_call x1, Pallas kernels, attention_fwd(): pl.pallas_call(functools.partial(fwd_kernel, (2, 1, 3, 0, 4), 2, scale *...  39.9 us
    ppermute x8, waiting for transfers between devices, passed_along(): return lax.ppermute(block, axis, route)  35.1 us
    all_gather x1, blocking collectives, per_device(): lax.all_gather(out_master.astype(bf16), 'node', axis=0, tiled=True)  34.8 us
    reduce_scatter x1, waiting for transfers between devices, per_device(): lax.psum_scatter(down_grad, 'node', scatter_dimension=0, tiled=True)  34.7 us
    reduce_scatter x1, waiting for transfers between devices, per_device(): lax.psum_scatter(qkv_grad, 'node', scatter_dimension=0, tiled=True)  30.1 us
  transfers between devices with their start and end apart: 15, of which 8 were waited for; matrix products, arithmetic and copies ran while one was open for 6% of the time, Pallas kernels for 3%

profile of v1, /device:TPU:0, one launch (start us, length us, event | category | flops | bytes accessed | tf_op | source)
XLA Modules:
  0.0 572.1 jit_solution(17597802099513331797)
XLA Ops:
  9.1 25.5 %psum.42 = f32[4,2048]{1,0:T(4,128)S(1)} all-reduce(f32[4,2048]{1,0:T(4,128)S(1)} %fusion.38), channel_id=1, replica_groups=mesh['head'=4,'node'=8] {'node'}, use_global_device_ids=true, to_apply=%region_4.5 | all-reduce | flops 8192 | bytes 65536 | tf_op jit(solution)/shard_map/psum | solution.py:230
  37.6 8.6 %all_gather.12 = bf16[512,384]{1,0:T(8,128)(2,1)S(1)} all-gather(bf16[64,384]{1,0:T(8,128)(2,1)S(1)} %convert_element_type.115), channel_id=1, replica_groups=mesh['head'=4,'node'=8] {'node'}, dimensions={0}, use_global_device_ids=true | all-gather | bytes 442368 | tf_op jit(solution)/shard_map/all_gather | solution.py:217
  46.2 3.5 fusion.34
  49.8 3.3 copy-done.2
  56.3 1.5 collective-permute-start
  57.9 2.6 collective-permute-start.2
  62.8 34.8 %all_gather.13 = bf16[128,512]{1,0:T(8,128)(2,1)S(1)} all-gather(bf16[16,512]{1,0:T(8,128)(2,1)S(1)} %convert_element_type.118), channel_id=1, replica_groups=mesh['head'=4,'node'=8] {'node'}, dimensions={0}, use_global_device_ids=true | all-gather | bytes 147456 | tf_op jit(solution)/shard_map/all_gather | solution.py:218
  102.8 1.6 copy-done.6
  104.4 39.9 %attend_fwd.1 = (f32[1024,128]{1,0:T(8,128)}, bf16[5,1024,1024]{2,1,0:T(8,128)(2,1)}, f32[1024,128]{1,0:T(8,128)}) custom-call(bf16[1024,128]{1,0:T(8,128)(2,1)} %slice.55.q, bf16[5,1024,256]{2,1,0:T(8,128)(2,1)} %copy-done.6, s32[64,256]{1,0:T(8,128)} %get-tuple-element.59.hik, s32[64,256]{1,0:T(8,128)} %get-tuple-element.58.lok), custom_call_target="tpu_custom_call" | custom-call | tf_op jit(solution)/shard_map/attend_fwd/pallas_call | solution.py:126
  144.3 2.5 convolution_convert_fusion
  146.9 10.9 %all_gather.14 = bf16[512,512]{1,0:T(8,128)(2,1)} all-gather(bf16[64,512]{1,0:T(8,128)(2,1)S(1)} %convert_element_type.122), channel_id=1, replica_groups=mesh['head'=4,'node'=8] {'node'}, dimensions={0}, use_global_device_ids=true | all-gather | bytes 589824 | tf_op jit(solution)/shard_map/all_gather | solution.py:219
  157.7 41.5 %all-reduce.5.cloned.1.call-done = bf16[1024,512]{1,0:T(8,128)(2,1)} async-done(((bf16[1024,512]{1,0:T(8,128)(2,1)}), bf16[1024,512]{1,0:T(8,128)(2,1)}) %all-reduce.5.cloned.1.call-update) | async-done | bytes 1048592 | tf_op jit(solution)/shard_map/psum | solution.py:252
  199.2 1.7 fusion.24
  202.1 2.9 fusion.21
  205.1 2.2 multiply_convert_fusion.1
  208.3 1.7 fusion.68
  210.8 34.7 %reduce-scatter.11.cloned.1.call-done = f32[64,512]{1,0:T(8,128)} async-done(((f32[512,512]{1,0:T(8,128)}), f32[64,512]{1,0:T(8,128)}) %reduce-scatter.11.cloned.1.call-update) | async-done | bytes 131088 | tf_op jit(solution)/shard_map/reduce_scatter | solution.py:317
  245.4 2.0 multiply_subtract_fusion.1
  247.4 9.8 %all_gather.15 = bf16[512,512]{1,0:T(8,128)(2,1)S(1)} all-gather(bf16[64,512]{1,0:T(8,128)(2,1)S(1)} %get-tuple-element.57), channel_id=1, replica_groups=mesh['head'=4,'node'=8] {'node'}, dimensions={0}, use_global_device_ids=true | all-gather | bytes 589824 | tf_op jit(solution)/shard_map/all_gather | solution.py:220
  257.2 3.0 multiply_convert_fusion
  261.2 1.7 convolution_convert_fusion.2
  263.0 52.0 %all-reduce.7.cloned.1.call-done = bf16[1024,512]{1,0:T(8,128)(2,1)} async-done(((bf16[1024,512]{1,0:T(8,128)(2,1)}), bf16[1024,512]{1,0:T(8,128)(2,1)}) %all-reduce.7.cloned.1.call-update) | async-done | bytes 1048592 | tf_op jit(solution)/shard_map/psum | solution.py:269
  314.9 3.0 fusion.36
  318.0 3.8 convert_multiply_fusion
  324.1 3.2 fusion.67
  327.7 2.8 convolution_convert_fusion.5.do
  330.4 16.9 %attend_bwd.1 = (f32[1024,128]{1,0:T(8,128)}, f32[5,256,1024]{2,1,0:T(8,128)}) custom-call(bf16[1024,128]{1,0:T(8,128)(2,1)} %slice.55.q, bf16[1024,128]{1,0:T(8,128)(2,1)} %convolution_convert_fusion.5.do, f32[1024,128]{1,0:T(8,128)} %get-tuple-element.22.att, f32[1024,128]{1,0:T(8,128)} %get-tuple-element.23.fac, bf16[5,1024,256]{2,1,0:T(8,128)(2,1)} %copy-done.6, ...), custom_call_target="tpu_custom_call" | custom-call | tf_op jit(solution)/shard_map/attend_bwd/pallas_call | solution.py:169
  347.3 2.9 convert.14
  351.6 2.4 collective-permute-start.4
  355.3 1.9 copy.47
  357.2 9.7 %collective-permute-done.4 = bf16[256,1024]{1,0:T(8,128)(2,1)} collective-permute-done((bf16[256,1024]{1,0:T(8,128)(2,1)}, bf16[256,1024]{1,0:T(8,128)(2,1)}, u32[]{:S(2)}, u32[]{:S(2)}) %collective-permute-start.4) | collective-permute-done | bytes 524320 | tf_op jit(solution)/shard_map/ppermute | solution.py:27
  366.9 10.9 %collective-permute-done.5 = bf16[256,1024]{1,0:T(8,128)(2,1)} collective-permute-done((bf16[256,1024]{1,0:T(8,128)(2,1)}, bf16[256,1024]{1,0:T(8,128)(2,1)}, u32[]{:S(2)}, u32[]{:S(2)}) %collective-permute-start.5) | collective-permute-done | bytes 524320 | tf_op jit(solution)/shard_map/ppermute | solution.py:27
  377.8 14.4 %collective-permute-done.7 = bf16[256,1024]{1,0:T(8,128)(2,1)} collective-permute-done((bf16[256,1024]{1,0:T(8,128)(2,1)}, bf16[256,1024]{1,0:T(8,128)(2,1)}, u32[]{:S(2)}, u32[]{:S(2)}) %collective-permute-start.7) | collective-permute-done | bytes 524320 | tf_op jit(solution)/shard_map/ppermute | solution.py:27
  392.2 2.3 fusion.30
  395.3 1.6 fusion.35
  397.3 3.1 convolution_convert_fusion.3
  400.4 1.8 convolution_convert_fusion.1
  402.3 1.6 convert_element_type.131
  403.9 1.4 multiply_subtract_fusion.4
  405.3 1.8 multiply_subtract_fusion.2
  407.1 30.1 %reduce-scatter.5.cloned.1.call-done = f32[64,384]{1,0:T(8,128)} async-done(((f32[512,384]{1,0:T(8,128)}), f32[64,384]{1,0:T(8,128)}) %reduce-scatter.5.cloned.1.call-update) | async-done | bytes 98320 | tf_op jit(solution)/shard_map/reduce_scatter | solution.py:314
  437.1 1.7 multiply_subtract_fusion.3
  438.9 87.4 %all-reduce.9.cloned.1.call-done = (bf16[1024,512]{1,0:T(8,128)(2,1)}, bf16[1024,512]{1,0:T(8,128)(2,1)}) async-done(((bf16[1024,512]{1,0:T(8,128)(2,1)}, bf16[1024,512]{1,0:T(8,128)(2,1)}), (bf16[1024,512]{1,0:T(8,128)(2,1)}, bf16[1024,512]{1,0:T(8,128)(2,1)})) %all-reduce.9.cloned.1.call-update) | async-done | bytes 2097168 | tf_op jit(solution)/shard_map/psum | solution.py:261
  526.3 3.2 fusion.37
  531.1 2.9 fusion
  533.9 23.7 %psum.47 = f32[4,2048]{1,0:T(4,128)S(1)} all-reduce(f32[4,2048]{1,0:T(4,128)S(1)} %fusion), channel_id=1, replica_groups=mesh['head'=4,'node'=8] {'node'}, use_global_device_ids=true, to_apply=%region_15.16 | all-reduce | flops 8192 | bytes 65536 | tf_op jit(solution)/shard_map/psum | solution.py:311
  557.6 3.5 multiply_subtract_fusion
  561.1 3.7 fusion.19
  (142 shorter events, 26.9 us)
Async XLA Ops:
  7.2 29.8 %copy-start.1 = (bf16[1024,512]{1,0:T(8,128)(2,1)S(1)}, bf16[1024,512]{1,0:T(8,128)(2,1)}, u32[]{:S(2)}) copy-start(bf16[1024,512]{1,0:T(8,128)(2,1)} %param.22) | copy-start | bytes 3145732
  7.2 30.3 %copy-start.27 = (f32[64,384]{1,0:T(8,128)S(1)}, f32[64,384]{1,0:T(8,128)}, u32[]{:S(2)}) copy-start(f32[64,384]{1,0:T(8,128)} %param.32) | copy-start | bytes 294916
  7.2 192.0 %all-reduce.5.cloned.1.call-start = ((), (), s32[]{:S(2)}) async-start(), calls=%async_computation.4 | async-start | bytes 2097152 | tf_op jit(solution)/shard_map/psum | solution.py:252
  37.5 12.2 %copy-start.33 = (f32[1024]{0:T(1024)}, f32[1024]{0:T(1024)S(1)}, u32[]{:S(2)}) copy-start(f32[1024]{0:T(1024)S(1)} %add_rsqrt_fusion.1) | copy-start | bytes 12292
  46.1 7.5 %copy-start.25 = (bf16[512,384]{1,0:T(8,128)(2,1)}, bf16[512,384]{1,0:T(8,128)(2,1)S(1)}, u32[]{:S(2)}) copy-start(bf16[512,384]{1,0:T(8,128)(2,1)S(1)} %all_gather.12) | copy-start | bytes 1179652
  49.8 3.3 copy-start.2
  54.7 6.3 %copy-start.36 = (s32[1024,16]{0,1:T(8,128)S(1)}, s32[1024,16]{0,1:T(8,128)}, u32[]{:S(2)}) copy-start(s32[1024,16]{0,1:T(8,128)} %param.25) | copy-start | bytes 196612
  54.7 6.4 %copy-start.35 = (s32[1024,16]{0,1:T(8,128)S(1)}, s32[1024,16]{0,1:T(8,128)}, u32[]{:S(2)}) copy-start(s32[1024,16]{0,1:T(8,128)} %param.26) | copy-start | bytes 196612
  55.4 42.9 %copy-start.10 = (bf16[1024,384]{1,0:T(8,128)(2,1)}, bf16[1024,384]{1,0:T(8,128)(2,1)S(1)}, u32[]{:S(2)}) copy-start(bf16[1024,384]{1,0:T(8,128)(2,1)S(1)} %convolution_convert_fusion.4) | copy-start | bytes 2359300
  55.4 7.4 %copy-start.31 = (f32[16,512]{1,0:T(8,128)S(1)}, f32[16,512]{1,0:T(8,128)}, u32[]{:S(2)}) copy-start(f32[16,512]{1,0:T(8,128)} %param.35) | copy-start | bytes 98308
  56.3 42.0 %collective-permute-start = (bf16[1024,256]{1,0:T(8,128)(2,1)}, bf16[1024,256]{1,0:T(8,128)(2,1)}, u32[]{:S(2)}, u32[]{:S(2)}) collective-permute-start(bf16[1024,256]{1,0:T(8,128)(2,1)} %slice.56), channel_id=1, source_target_pairs={{6,0},{7,1},{0,2},{1,3},{2,4},{3,5},{4,6},{5,7},{14,8},{15,9},{8,1... | collective-permute-start | bytes 1572872 | tf_op jit(solution)/shard_map/ppermute | solution.py:27
  57.9 41.6 %collective-permute-start.1 = (bf16[1024,256]{1,0:T(8,128)(2,1)}, bf16[1024,256]{1,0:T(8,128)(2,1)}, u32[]{:S(2)}, u32[]{:S(2)}) collective-permute-start(bf16[1024,256]{1,0:T(8,128)(2,1)} %slice.56), channel_id=1, source_target_pairs={{7,0},{0,1},{1,2},{2,3},{3,4},{4,5},{5,6},{6,7},{15,8},{8,9},{9,10... | collective-permute-start | bytes 1572872 | tf_op jit(solution)/shard_map/ppermute | solution.py:27
  57.9 42.7 %collective-permute-start.2 = (bf16[1024,256]{1,0:T(8,128)(2,1)}, bf16[1024,256]{1,0:T(8,128)(2,1)}, u32[]{:S(2)}, u32[]{:S(2)}) collective-permute-start(bf16[1024,256]{1,0:T(8,128)(2,1)} %slice.56), channel_id=1, source_target_pairs={{1,0},{2,1},{3,2},{4,3},{5,4},{6,5},{7,6},{0,7},{9,8},{10,9},{11,1... | collective-permute-start | bytes 1572872 | tf_op jit(solution)/shard_map/ppermute | solution.py:27
  60.5 41.2 %collective-permute-start.3 = (bf16[1024,256]{1,0:T(8,128)(2,1)}, bf16[1024,256]{1,0:T(8,128)(2,1)}, u32[]{:S(2)}, u32[]{:S(2)}) collective-permute-start(bf16[1024,256]{1,0:T(8,128)(2,1)} %slice.56), channel_id=1, source_target_pairs={{2,0},{3,1},{4,2},{5,3},{6,4},{7,5},{0,6},{1,7},{10,8},{11,9},{12,... | collective-permute-start | bytes 1572872 | tf_op jit(solution)/shard_map/ppermute | solution.py:27
  98.4 2.3 copy-start.11
  102.8 1.6 copy-start.6
  144.3 2.5 copy-start.21
  146.8 98.6 %reduce-scatter.11.cloned.1.call-start = ((), (), s32[]{:S(2)}) async-start(), calls=%async_computation.9 | async-start | bytes 1179648 | tf_op jit(solution)/shard_map/reduce_scatter | solution.py:317
  199.2 1.7 copy-start.3
  202.1 2.9 copy-start.23
  205.1 2.3 copy-start.17
  205.1 3.2 copy-start.14
  210.0 104.9 %all-reduce.7.cloned.1.call-start = ((), (), s32[]{:S(2)}) async-start(), calls=%async_computation.5 | async-start | bytes 2097152 | tf_op jit(solution)/shard_map/psum | solution.py:269
  257.2 3.0 copy-start.22
  257.2 4.0 copy-start.24
  262.9 141.0 %reduce-scatter.7.cloned.1.call-start = ((), (), s32[]{:S(2)}) async-start(), calls=%async_computation.7 | async-start | bytes 294912 | tf_op jit(solution)/shard_map/reduce_scatter | solution.py:315
  314.9 3.0 copy-start.7
  318.0 5.1 copy-start.9
  321.7 1.3 copy-start.4
  324.1 81.2 %reduce-scatter.9.cloned.1.call-start = ((), (), s32[]{:S(2)}) async-start(), calls=%async_computation.8 | async-start | bytes 1179648 | tf_op jit(solution)/shard_map/reduce_scatter | solution.py:316
  327.4 109.7 %reduce-scatter.5.cloned.1.call-start = ((), (), s32[]{:S(2)}) async-start(), calls=%async_computation.6 | async-start | bytes 884736 | tf_op jit(solution)/shard_map/reduce_scatter | solution.py:314
  351.6 15.3 %collective-permute-start.4 = (bf16[256,1024]{1,0:T(8,128)(2,1)}, bf16[256,1024]{1,0:T(8,128)(2,1)}, u32[]{:S(2)}, u32[]{:S(2)}) collective-permute-start(bf16[256,1024]{1,0:T(8,128)(2,1)} %get-tuple-element.50), channel_id=1, source_target_pairs={{2,0},{3,1},{4,2},{5,3},{6,4},{7,5},{0,6},{1,7},{10,8},{11,9},{12,... | collective-permute-start | bytes 1572872 | tf_op jit(solution)/shard_map/ppermute | solution.py:27
  354.0 23.9 %collective-permute-start.5 = (bf16[256,1024]{1,0:T(8,128)(2,1)}, bf16[256,1024]{1,0:T(8,128)(2,1)}, u32[]{:S(2)}, u32[]{:S(2)}) collective-permute-start(bf16[256,1024]{1,0:T(8,128)(2,1)} %get-tuple-element.53), channel_id=1, source_target_pairs={{1,0},{2,1},{3,2},{4,3},{5,4},{6,5},{7,6},{0,7},{9,8},{10,9},{11,1... | collective-permute-start | bytes 1572872 | tf_op jit(solution)/shard_map/ppermute | solution.py:27
  354.0 23.9 %collective-permute-start.6 = (bf16[256,1024]{1,0:T(8,128)(2,1)}, bf16[256,1024]{1,0:T(8,128)(2,1)}, u32[]{:S(2)}, u32[]{:S(2)}) collective-permute-start(bf16[256,1024]{1,0:T(8,128)(2,1)} %get-tuple-element.52), channel_id=1, source_target_pairs={{7,0},{0,1},{1,2},{2,3},{3,4},{4,5},{5,6},{6,7},{15,8},{8,9},{9,10... | collective-permute-start | bytes 1572872 | tf_op jit(solution)/shard_map/ppermute | solution.py:27
  354.5 37.7 %collective-permute-start.7 = (bf16[256,1024]{1,0:T(8,128)(2,1)}, bf16[256,1024]{1,0:T(8,128)(2,1)}, u32[]{:S(2)}, u32[]{:S(2)}) collective-permute-start(bf16[256,1024]{1,0:T(8,128)(2,1)} %get-tuple-element.51), channel_id=1, source_target_pairs={{6,0},{7,1},{0,2},{1,3},{2,4},{3,5},{4,6},{5,7},{14,8},{15,9},{8,1... | collective-permute-start | bytes 1572872 | tf_op jit(solution)/shard_map/ppermute | solution.py:27
  357.1 38.1 %copy-start.16 = (bf16[1024,512]{1,0:T(8,128)(2,1)S(1)}, bf16[1024,512]{1,0:T(8,128)(2,1)}, u32[]{:S(2)}) copy-start(bf16[1024,512]{1,0:T(8,128)(2,1)} %copy-done.15) | copy-start | bytes 3145732
  357.1 38.1 %copy-start.28 = (bf16[1024,128]{0,1:T(8,128)(2,1)S(1)}, bf16[1024,128]{0,1:T(8,128)(2,1)}, u32[]{:S(2)}) copy-start(bf16[1024,128]{0,1:T(8,128)(2,1)} %copy.47) | copy-start | bytes 786436
  397.0 129.3 %all-reduce.9.cloned.1.call-start = ((), (), s32[]{:S(2)}) async-start(), calls=%async_computation.10 | async-start | bytes 4194304 | tf_op jit(solution)/shard_map/psum | solution.py:261
  397.3 3.2 copy-start.20
  397.3 3.2 copy-start.26
  397.3 3.2 copy-start.29
  402.2 3.1 copy-start.30
  402.3 124.0 %copy-start.34 = (f32[1024]{0:T(1024)S(1)}, f32[1024]{0:T(1024)}, u32[]{:S(2)}) copy-start(f32[1024]{0:T(1024)} %copy-done.33) | copy-start | bytes 12292
  526.3 3.2 copy-start.8
  526.3 3.5 copy-start.13
  529.5 1.6 copy-start.12
  557.6 3.5 copy-start.5
  557.6 3.5 copy-start.18
  (6 other events, 5.1 us)
Sparse Core Ops, SparseCore 0:
  146.9 52.2 all-reduce.4
  210.2 35.2 reduce-scatter.10
  263.0 51.8 all-reduce.6
  324.2 33.0 reduce-scatter.6
  360.3 38.7 reduce-scatter.8
  402.1 34.9 reduce-scatter.4
  440.1 86.1 all-reduce.8

commit v2 on v1

--- a/solution.py
+++ b/solution.py
@@ -7,7 +7,6 @@
 from jax.experimental import pallas as pl
 from jax.experimental.pallas import tpu as pltpu
 from jax.sharding import PartitionSpec as P
-
 
 WIDTH = 512
 HIDDEN_SIZE = 2048
@@ -52,17 +51,15 @@
 NT=(((1,),(1,)),((),()))
 SPAN=256
 
-def count_groups(cnt, hik, lok, rows):
-    steps=hik.shape[0]
+def count_groups(cnt, hik, lok, rows, start, stop):
     parts=rows//SPAN
     total=5*parts*16
     rowid=lax.broadcasted_iota(jnp.int32,(total,1),0)
-    rowkey=lax.div(rowid,16)*16+lax.rem(rowid,16)
     spot=lax.broadcasted_iota(jnp.int32,(SPAN,1),0)
     def body(g,_):
         keys=hik[pl.ds(g,1),:]
         low=lok[pl.ds(g,1),:]
-        left=jnp.where(rowkey==keys,1.0,0.0).astype(bf16)
+        left=jnp.where(rowid==keys,1.0,0.0).astype(bf16)
         right=jnp.where(spot==low,1.0,0.0).astype(bf16)
         made=lax.dot_general(left,right,NT,preferred_element_type=f32).astype(bf16)
         at=pl.multiple_of(g*16,16)
@@ -71,7 +68,7 @@
                 r=(b*parts+p)*16
                 cnt[b,pl.ds(at,16),p*SPAN:(p+1)*SPAN]=made[r:r+16,:]
         return 0
-    lax.fori_loop(0,steps,body,0)
+    lax.fori_loop(start,stop,body,0)
 
 def add_self(cnt, block, rows):
     eye=(lax.broadcasted_iota(jnp.int32,(SPAN,SPAN),0)==lax.broadcasted_iota(jnp.int32,(SPAN,SPAN),1))
@@ -111,7 +108,7 @@
 
 def fwd_kernel(order, self_block, scale, q, kv, hik, lok, att, e, fac, cnt, m, l):
     rows=q.shape[0]
-    count_groups(cnt,hik,lok,rows)
+    count_groups(cnt,hik,lok,rows,0,hik.shape[0])
     add_self(cnt,self_block,rows)
     for t,b in enumerate(order):
         attend_block(b,t==0,q,kv[b,:,:128],kv[b,:,128:],cnt,e,m,l,att,fac,256,scale)
@@ -129,15 +126,13 @@
         scratch_shapes=[V((5,rows,rows),bf16),V((rows,128),f32),V((rows,128),f32)],
         compiler_params=pltpu.CompilerParams(vmem_limit_bytes=60<<20),name="attend_fwd")(q,kv,hik,lok)
 
-def back_block(b, q_t, do, fac, delta, kv, e, dq, dkv, first, chunk, keyscale):
+def back_block(b, q_t, do, fac, delta, kv, e, dq, write, first, chunk, keyscale):
     rows=do.shape[0]
     f=fac[:,b:b+1]
-    dob=(do*f)
-    dobh=dob.astype(bf16)
+    dobh=(do*f).astype(bf16)
     d=-(delta*f)
     h=d.astype(bf16); r=d-h.astype(f32); h2=r.astype(bf16); h3=(r-h2.astype(f32)).astype(bf16)
     lane=lax.broadcasted_iota(jnp.int32,(rows,128),1)
-    zero=jnp.zeros((rows,128),bf16)
     dcol=jnp.where(lane==0,h.astype(f32),jnp.where(lane==1,h2.astype(f32),jnp.where(lane==2,h3.astype(f32),0.0))).astype(bf16)
     left=jnp.concatenate([dobh,dcol],axis=1)
     dob_t=dobh.T
@@ -148,8 +143,8 @@
         dp=lax.dot_general(left,right,NT,preferred_element_type=f32)
         w=e[b,:,s]
         ds=(dp*w.astype(f32)).astype(bf16)
-        dkv[b,:128,s]=jnp.dot(q_t,ds,preferred_element_type=f32)*keyscale
-        dkv[b,128:,s]=jnp.dot(dob_t,w,preferred_element_type=f32)
+        write(slice(0,128),s,jnp.dot(q_t,ds,preferred_element_type=f32)*keyscale)
+        write(slice(128,256),s,jnp.dot(dob_t,w,preferred_element_type=f32))
         out=jnp.dot(ds,kv[b,s,:128],preferred_element_type=f32)
         if first and i==0: dq[...]=out
         else: dq[...]+=out
@@ -159,7 +154,8 @@
     dof=do[...].astype(f32)
     delta=jnp.sum(dof*att[...],axis=1,keepdims=True)
     for t,b in enumerate((0,4,1,3,2)):
-        back_block(b,q_t,dof,fac,delta,kv,e,dq,dkv,t==0,512,scale)
+        def write(r,s,v,b=b): dkv[b,r,s]=v
+        back_block(b,q_t,dof,fac,delta,kv,e,dq,write,t==0,512,scale)
     dq[...]=dq[...]*scale
 
 def attention_bwd(q,do,att,fac,kv,e,scale):
@@ -179,6 +175,444 @@
     hi=jnp.where(ok,(flat//SPAN)*16+node,-1)
     lo=flat%SPAN
     return hi,lo
+
+
+def by_batch(pos, limits, table, row, lanes):
+    pick=[table[row+b:row+b+1,lanes] for b in range(4)]
+    out=jnp.where(pos>=limits[0],pick[1],pick[0])
+    out=jnp.where(pos>=limits[1],pick[2],out)
+    return jnp.where(pos>=limits[2],pick[3],out)
+
+
+def batch_limits(counts):
+    return (counts[0],counts[0]+counts[1],counts[0]+counts[1]+counts[2])
+
+
+class Links:
+    def __init__(self, send, recv):
+        self.send, self.recv, self.used = send, recv, 0
+
+    def copy(self, src, dst, head, node):
+        made=pltpu.make_async_remote_copy(src_ref=src,dst_ref=dst,send_sem=self.send.at[self.used],recv_sem=self.recv.at[self.used],
+            device_id=(head,node),device_id_type=pl.DeviceIdType.MESH)
+        self.used+=1
+        return made
+
+
+def meet(peers):
+    barrier=pltpu.get_barrier_semaphore()
+    for head,node in peers:
+        pl.semaphore_signal(barrier,inc=1,device_id=(head,node),device_id_type=pl.DeviceIdType.MESH)
+    pl.semaphore_wait(barrier,len(peers))
+
+
+def front_kernel(scale, node_input, sigma, ada, qkv, out, up, down, counts, hik, lok,
+        att, fac, queries, table, xn_one, modulation, qkv_full, out_full, up_full, down_full, e_out,
+        e, cnt, m, l, normed, modp, modbuf, send, recv, store):
+    head=lax.axis_index("head"); node=lax.axis_index("node")
+    rows=node_input.shape[0]
+    chunk=rows//4
+    links=Links(send,recv)
+    meet([(head,node^k) for k in range(1,8)]+[(head^k,node) for k in range(1,4)])
+    limits=batch_limits(counts)
+    own=pl.ds(pl.multiple_of(node*64,64),64)
+    qkv_full[own,:]=qkv[...].astype(bf16)
+    part=jnp.dot(sigma[...],ada[...].astype(bf16),preferred_element_type=f32)
+    modp[0:4,:]=part[:,:1024]
+    modp[4:8,:]=part[:,1024:]
+    first=[]
+    for k in range(1,8):
+        first.append(links.copy(modp,modbuf.at[node],head,node^k)); first[-1].start()
+        first.append(links.copy(qkv_full.at[own],qkv_full.at[own],head,node^k)); first[-1].start()
+    cols=pl.ds(pl.multiple_of(head*512,512),512)
+    own_out=pl.ds(pl.multiple_of(node*16,16),16)
+    up_full[own,cols]=up[...].astype(bf16)
+    down_full[head,own,:]=down[...].astype(bf16)
+    out_full[head,own_out,:]=out[...].astype(bf16)
+    along=[]
+    for k in range(1,4):
+        for ref in (up_full.at[own,cols],down_full.at[head,own],out_full.at[head,own_out]):
+            along.append(links.copy(ref,ref,head^k,node)); along[-1].start()
+    modbuf[node,:,:]=modp[...]
+    def norm(i,_):
+        at=pl.ds(pl.multiple_of(i*128,128),128)
+        v=node_input[at,:].astype(f32)
+        centred=v-jnp.mean(v,axis=1,keepdims=True)
+        normed[at,:]=centred*lax.rsqrt(jnp.mean(centred*centred,axis=1,keepdims=True)+norm_eps)
+        return 0
+    lax.fori_loop(0,rows//128,norm,0)
+    for c in first: c.wait()
+    mod=modbuf[0]
+    for k in range(1,8): mod=mod+modbuf[k]
+    modulation[...]=mod
+    across=[]; paired=[]
+    for i in range(4):
+        at=slice(i*chunk,(i+1)*chunk)
+        pos=node*rows+i*chunk+lax.broadcasted_iota(jnp.int32,(chunk,1),0)
+        xn=(normed[at,:]*(1.0+by_batch(pos,limits,modulation,0,slice(0,512)))+by_batch(pos,limits,modulation,0,slice(512,1024))).astype(bf16)
+        xn_one[at,:]=xn
+        proj=jnp.dot(xn,qkv_full[...],preferred_element_type=f32).astype(bf16)
+        queries[at,:]=proj[:,:128]
+        table[0,at,:]=proj[:,128:]
+        across.append(links.copy(table.at[0,at],table.at[2,at],head,node^2)); across[-1].start()
+        paired.append(links.copy(table.at[0,at],table.at[1,at],head,node^1)); paired[-1].start()
+    onward=[]
+    steps=hik.shape[0]
+    def column(which):
+        at=pl.ds(pl.multiple_of((node^which)*64,64),64); at_out=pl.ds(pl.multiple_of((node^which)*16,16),16)
+        return [up_full.at[at],down_full.at[:,at],out_full.at[:,at_out]]
+    for i in range(4):
+        count_groups(cnt,hik,lok,rows,i*steps//4,(i+1)*steps//4)
+        across[i].wait_recv()
+        at=slice(i*chunk,(i+1)*chunk)
+        onward.append(links.copy(table.at[2,at],table.at[3,at],head,node^4)); onward[-1].start()
+        if i==2:
+            for c in along: c.wait()
+            mine=column(0)
+            to_pair=[links.copy(r,r,head,node^1) for r in mine]
+            to_x=[links.copy(r,r,head,node^2) for r in mine]
+            to_y=[links.copy(r,r,head,node^4) for r in mine]
+            for c in to_x+to_y+to_pair: c.start()
+    add_self(cnt,0,rows)
+    for c in across: c.wait_send()
+    saved=[]
+    def block(b,t):
+        attend_block(b,t==0,queries,table[b,:,:128],table[b,:,128:],cnt,e,m,l,att,fac,256,scale)
+        saved.append(pltpu.make_async_copy(e.at[b],e_out.at[b],store.at[b])); saved[-1].start()
+    block(0,0)
+    for c in paired: c.wait()
+    block(1,1)
+    for c in to_x: c.wait()
+    for c in to_y: c.wait()
+    from_x=column(2); from_y=column(4)
+    cross=[links.copy(from_x[0],from_x[0],head,node^4)]+[links.copy(r,r,head,node^2) for r in from_y[1:]]
+    for c in cross: c.start()
+    hand=[links.copy(r,r,head,node^1) for r in from_x+from_y]
+    for c in hand: c.start()
+    for c in onward: c.wait()
+    x_at=(node//2)%2; core=node%2
+    fifth=links.copy(table.at[jnp.where(x_at==core,2,3)],table.at[4],head,node^1)
+    fifth.start()
+    block(2,2)
+    block(3,3)
+    for c in cross: c.wait()
+    last=[links.copy(r,r,head,node^1) for r in column(6)]
+    for c in last: c.start()
+    fifth.wait()
+    block(4,4)
+    inv=1.0/l[...]
+    att[...]=att[...]*inv
+    fac[...]=jnp.exp2(fac[...]-m[...])*inv
+    for c in to_pair+hand+last: c.wait()
+    for c in saved: c.wait()
+
+
+def front(node_input,sigma,ada,qkv,out,up,down,counts,hik,lok,scale):
+    rows=node_input.shape[0]
+    V=pltpu.VMEM
+    full=pl.BlockSpec(memory_space=V)
+    S=jax.ShapeDtypeStruct
+    copies=14+9+8+4+9+9+1+3
+    return pl.pallas_call(functools.partial(front_kernel,scale*math.log2(math.e)),
+        out_shape=(S((rows,128),f32),S((rows,128),f32),S((rows,128),bf16),S((5,rows,256),bf16),S((rows,512),bf16),S((8,1024),f32),
+            S((512,384),bf16),S((4,128,512),bf16),S((512,2048),bf16),S((4,512,512),bf16),S((5,rows,rows),bf16)),
+        in_specs=[full]*7+[pl.BlockSpec(memory_space=pltpu.SMEM)]+[full]*2,
+        out_specs=(full,)*10+(pl.BlockSpec(memory_space=pl.ANY),),
+        scratch_shapes=[V((5,rows,rows),bf16),V((5,rows,rows),bf16),V((rows,128),f32),V((rows,128),f32),V((rows,512),f32),
+            V((8,1024),f32),V((8,8,1024),f32),pltpu.SemaphoreType.DMA((copies,)),pltpu.SemaphoreType.DMA((copies,)),pltpu.SemaphoreType.DMA((5,))],
+        compiler_params=pltpu.CompilerParams(vmem_limit_bytes=62<<20,collective_id=1,has_side_effects=True),
+        name="front")(node_input,sigma,ada,qkv,out,up,down,counts,hik,lok)
+
+
+def slots(neighbours, valid, node, rows):
+    flat=neighbours.reshape(-1,256)
+    ok=(valid>0).reshape(-1,256)
+    which=(flat//rows)^node
+    slot=jnp.where(which==6,3,jnp.where((which==3)|(which==7),4,which))
+    local=flat%rows
+    spot=lax.broadcasted_iota(jnp.int32,flat.shape,1)//16
+    hi=jnp.where(ok,(slot*(rows//SPAN)+local//SPAN)*16+spot,-1)
+    return hi,local%SPAN
+
+
+def batch_sums(pos, limits, values):
+    lane=lax.broadcasted_iota(jnp.int32,(pos.shape[0],8),1)
+    member=(pos>=limits[0]).astype(jnp.int32)+(pos>=limits[1]).astype(jnp.int32)+(pos>=limits[2]).astype(jnp.int32)
+    onehot=jnp.where(lane==member,1.0,0.0).astype(f32)
+    return lax.dot_general(onehot,values,(((0,),(0,)),((),())),precision=highest,preferred_element_type=f32)[0:4,:]
+
+
+def middle_kernel(node_input, cotangent, att, modulation, counts, out_full, up_full, down_full,
+        do, dy, out_rows, up_grad, down_grad, out_grad, dmod,
+        mixed, heads, do_rows, act, pre, send, recv):
+    head=lax.axis_index("head"); node=lax.axis_index("node")
+    rows=node_input.shape[0]
+    part=rows//4
+    links=Links(send,recv)
+    mixed[...]=att[...].astype(bf16)
+    meet([(head^k,node) for k in range(1,4)])
+    lanes=pl.ds(pl.multiple_of(head*128,128),128)
+    mine=pl.ds(pl.multiple_of(head*part,part),part)
+    moved=[]
+    for k in range(1,4):
+        moved.append(links.copy(mixed.at[pl.ds(pl.multiple_of((head^k)*part,part),part)],heads.at[:,lanes],head^k,node)); moved[-1].start()
+    heads[:,lanes]=mixed[mine,:]
+    limits=batch_limits(counts)
+    pos=node*rows+head*part+lax.broadcasted_iota(jnp.int32,(part,1),0)
+    scale_two=1.0+by_batch(pos,limits,modulation,4,slice(0,512))
+    shift_two=by_batch(pos,limits,modulation,4,slice(512,1024))
+    g=cotangent[mine,:]
+    for c in moved: c.wait()
+    out_all=out_full[...].reshape(512,512)
+    y=node_input[mine,:].astype(f32)+jnp.dot(heads[...],out_all,preferred_element_type=f32)
+    n_two,inv_two=norm_parts(y)
+    xn=(n_two*scale_two+shift_two).astype(bf16)
+    mlp=jnp.zeros((part,512),f32); dxn=jnp.zeros((part,512),f32)
+    for j in range(4):
+        s=slice(j*512,(j+1)*512)
+        h=jnp.dot(xn,up_full[:,s],preferred_element_type=f32)
+        sig=1.0/(1.0+jnp.exp(-h))
+        u=(h*sig).astype(bf16)
+        act[:,s]=u
+        mlp+=jnp.dot(u,down_full[j],preferred_element_type=f32)
+        du=lax.dot_general(g,down_full[j],NT,preferred_element_type=f32)
+        d=(du*sig*(1.0+h*(1.0-sig))).astype(bf16)
+        pre[:,s]=d
+        dxn+=lax.dot_general(d,up_full[:,s],NT,preferred_element_type=f32)
+    dyv=g.astype(f32)+norm_back(dxn*scale_two,n_two,inv_two)
+    dy[...]=dyv
+    da=dyv.astype(bf16)
+    do_rows[...]=lax.dot_general(da,out_all,NT,preferred_element_type=f32).astype(bf16)
+    back=[]
+    for k in range(1,4):
+        back.append(links.copy(do_rows.at[:,pl.ds(pl.multiple_of((head^k)*128,128),128)],do.at[mine],head^k,node)); back[-1].start()
+    do[mine,:]=do_rows[:,lanes]
+    out_rows[...]=(y+mlp).astype(bf16)
+    dmod[0:4,:]=jnp.zeros((4,1024),f32)
+    dmod[4:8,0:512]=batch_sums(pos,limits,dxn*n_two)
+    dmod[4:8,512:1024]=batch_sums(pos,limits,dxn)
+    xn_t=xn.T
+    heads_t=heads[...].T
+    out_grad[...]=jnp.dot(heads_t,da,preferred_element_type=f32).astype(bf16).reshape(4,128,512)
+    for j in range(4):
+        s=slice(j*512,(j+1)*512)
+        up_grad[:,s]=jnp.dot(xn_t,pre[:,s],preferred_element_type=f32).astype(bf16)
+        down_grad[j]=jnp.dot(act[:,s].T,g,preferred_element_type=f32).astype(bf16)
+    for c in back: c.wait()
+
+
+def middle(node_input,cotangent,att,modulation,counts,out_full,up_full,down_full):
+    rows=node_input.shape[0]
+    part=rows//4
+    V=pltpu.VMEM
+    full=pl.BlockSpec(memory_space=V)
+    S=jax.ShapeDtypeStruct
+    return pl.pallas_call(middle_kernel,
+        out_shape=(S((rows,128),bf16),S((part,512),f32),S((part,512),bf16),S((512,2048),bf16),S((4,512,512),bf16),S((4,128,512),bf16),S((8,1024),f32)),
+        in_specs=[full]*4+[pl.BlockSpec(memory_space=pltpu.SMEM)]+[full]*3,
+        out_specs=(full,)*7,
+        scratch_shapes=[V((rows,128),bf16),V((part,512),bf16),V((part,512),bf16),V((part,2048),bf16),V((part,2048),bf16),
+            pltpu.SemaphoreType.DMA((6,)),pltpu.SemaphoreType.DMA((6,))],
+        compiler_params=pltpu.CompilerParams(vmem_limit_bytes=62<<20,collective_id=2,has_side_effects=True),
+        name="middle")(node_input,cotangent,att,modulation,counts,out_full,up_full,down_full)
+
+
+def back_kernel(scale, queries, do, att, fac, table, xn_one, qkv_full, dy, node_input, modulation, counts, out_rows,
+        up_grad, down_grad, out_grad, dmod, e_in,
+        node_output, input_grad, up_sum, down_sum, out_sum, qkv_sum, dmod_sum,
+        e, dq, dkv, near, got_pair, got_y, got_x, got_one, proj_grad, partial, got_partial, rows_grad, row_all,
+        up1, down1, out1, up2, down2, out2, up3, down3, out3, up_z, down_z, out_z, qkv_grad, qkv_got, dm_z, dm_own, dm_n,
+        send, recv, load):
+    head=lax.axis_index("head"); node=lax.axis_index("node")
+    y_at=node//4; x_at=(node//2)%2; core=node%2
+    rows=queries.shape[0]
+    part=rows//4
+    links=Links(send,recv)
+    loads=[pltpu.make_async_copy(e_in.at[b],e.at[b],load.at[b]) for b in range(5)]
+    order=(4,3,2,1,0)
+    for b in order: loads[b].start()
+    meet([(head,node^k) for k in range(1,8)]+[(head^k,node) for k in range(1,4)])
+    mine=pl.ds(pl.multiple_of(head*part,part),part)
+    shown=[]
+    for k in range(1,4):
+        shown.append(links.copy(out_rows,node_output.at[mine],head^k,node)); shown[-1].start()
+    node_output[mine,:]=out_rows[...]
+    stage1=[links.copy(up_grad.at[:,1-core],up1,head,node^1),links.copy(down_grad.at[:,:,1-core],down1,head,node^1),links.copy(out_grad.at[:,:,1-core],out1,head,node^1)]
+    for c in stage1: c.start()
+    q_t=queries[...].T
+    dof=do[...].astype(f32)
+    delta=jnp.sum(dof*att[...],axis=1,keepdims=True)
+    def block(b):
+        loads[b].wait()
+        def write(r,s,v):
+            if b==0: dkv[r,s]=v
+            else: near[b,r,s]=v.astype(bf16)
+        back_block(b,q_t,dof,fac,delta,table,e,dq,write,b==order[0],512,scale)
+    block(4)
+    give=links.copy(near.at[4],got_pair,head,node^1); give.start()
+    block(3)
+    give.wait()
+    @pl.when(x_at!=core)
+    def _(): near[3]=(near[3].astype(f32)+got_pair[...].astype(f32)).astype(bf16)
+    via_y=[]
+    for i in range(4):
+        s=slice(i*part,(i+1)*part)
+        via_y.append(links.copy(near.at[3,:,s],got_y.at[:,s],head,node^4)); via_y[-1].start()
+    for c in stage1: c.wait()
+    for i in range(4):
+        up1[i]=(up1[i].astype(f32)+up_grad[i,core].astype(f32)).astype(bf16)
+        down1[i]=(down1[i].astype(f32)+down_grad[i,:,core].astype(f32)).astype(bf16)
+        out1[i]=(out1[i].astype(f32)+out_grad[i,:,core].astype(f32)).astype(bf16)
+    stage2=[]
+    for i in range(2):
+        stage2.append(links.copy(up1.at[i*2+1-x_at],up2.at[i],head,node^2))
+    there=pl.ds((1-y_at)*2,2)
+    stage2+=[links.copy(down1.at[:,there],down2,head,node^4),links.copy(out1.at[:,there],out2,head,node^4)]
+    for c in stage2: c.start()
+    block(2)
+    @pl.when(x_at==core)
+    def _(): near[2]=(near[2].astype(f32)+got_pair[...].astype(f32)).astype(bf16)
+    via_x=[]
+    def pass_on(i):
+        s=slice(i*part,(i+1)*part)
+        via_y[i].wait()
+        near[2,:,s]=(near[2,:,s].astype(f32)+got_y[:,s].astype(f32)).astype(bf16)
+        via_x.append(links.copy(near.at[2,:,s],got_x.at[:,s],head,node^2)); via_x[-1].start()
+    pass_on(0)
+    block(1)
+    one=links.copy(near.at[1],got_one,head,node^1); one.start()
+    pass_on(1)
+    pass_on(2)
+    block(0)
+    pass_on(3)
+    for c in stage2: c.wait()
+    for i in range(2):
+        up2[i]=(up2[i].astype(f32)+up1[i*2+x_at].astype(f32)).astype(bf16)
+    here=pl.ds(y_at*2,2)
+    down2[...]=(down2[...].astype(f32)+down1[:,here].astype(f32)).astype(bf16)
+    out2[...]=(out2[...].astype(f32)+out1[:,here].astype(f32)).astype(bf16)
+    stage3=[links.copy(up2.at[1-y_at],up3,head,node^4),links.copy(down2.at[:,1-x_at],down3,head,node^2),links.copy(out2.at[:,1-x_at],out3,head,node^2)]
+    for c in stage3: c.start()
+    xn_t=xn_one[...].T
+    one.wait()
+    for i in range(4):
+        s=slice(i*part,(i+1)*part)
+        via_x[i].wait()
+        total=dkv[:,s]+got_one[:,s].astype(f32)+got_x[:,s].astype(f32)
+        proj_grad[s,128:]=total.T.astype(bf16)
+        proj_grad[s,:128]=(dq[s,:]*scale).astype(bf16)
+        partial[i]=lax.dot_general(proj_grad[s,:],qkv_full[...],NT,preferred_element_type=f32).astype(bf16)
+    reduce=[]
+    for k in range(1,4):
+        reduce.append(links.copy(partial.at[head^k],got_partial.at[k-1],head^k,node)); reduce[-1].start()
+    made=jnp.dot(xn_t,proj_grad[...],preferred_element_type=f32).astype(bf16)
+    qkv_grad[...]=made.reshape(8,64,384)
+    qkv_moves=[]
+    for k in range(1,8):
+        qkv_moves.append(links.copy(qkv_grad.at[node^k],qkv_got.at[k-1],head,node^k)); qkv_moves[-1].start()
+    for c in stage3: c.wait()
+    up3[...]=(up3[...].astype(f32)+up2[y_at].astype(f32)).astype(bf16)
+    down3[...]=(down3[...].astype(f32)+down2[:,x_at].astype(f32)).astype(bf16)
+    out3[...]=(out3[...].astype(f32)+out2[:,x_at].astype(f32)).astype(bf16)
+    stage4=[]
+    for k in range(1,4):
+        cols=pl.ds(pl.multiple_of((head^k)*512,512),512)
+        stage4+=[links.copy(up3.at[:,cols],up_z.at[k-1],head^k,node),links.copy(down3.at[head^k],down_z.at[k-1],head^k,node),links.copy(out3.at[head^k],out_z.at[k-1],head^k,node)]
+    limits=batch_limits(counts)
+    pos=node*rows+head*part+lax.broadcasted_iota(jnp.int32,(part,1),0)
+    scale_one=1.0+by_batch(pos,limits,modulation,0,slice(0,512))
+    n_one,inv_one=norm_parts(node_input[mine,:].astype(f32))
+    for c in reduce: c.wait()
+    dxn=partial[head].astype(f32)
+    for k in range(3): dxn=dxn+got_partial[k].astype(f32)
+    rows_grad[...]=(dy[...]+norm_back(dxn*scale_one,n_one,inv_one)).astype(bf16)
+    spread=[]
+    for k in range(1,4):
+        spread.append(links.copy(rows_grad,row_all.at[head],head^k,node)); spread[-1].start()
+    row_all[head,:,:]=rows_grad[...]
+    dm_own[0:4,0:512]=batch_sums(pos,limits,dxn*n_one)
+    dm_own[0:4,512:1024]=batch_sums(pos,limits,dxn)
+    dm_own[4:8,:]=dmod[4:8,:]
+    dm_moves=[]
+    for k in range(1,4):
+        dm_moves.append(links.copy(dm_own,dm_z.at[head],head^k,node)); dm_moves[-1].start()
+    dm_z[head,:,:]=dm_own[...]
+    for c in stage4: c.start()
+    for c in dm_moves: c.wait()
+    dm_own[...]=dm_z[0]+dm_z[1]+dm_z[2]+dm_z[3]
+    dm_last=[]
+    for k in range(1,8):
+        dm_last.append(links.copy(dm_own,dm_n.at[node],head,node^k)); dm_last[-1].start()
+    dm_n[node,:,:]=dm_own[...]
+    for c in qkv_moves: c.wait()
+    total=qkv_grad[node].astype(f32)
+    for k in range(7): total=total+qkv_got[k].astype(f32)
+    qkv_sum[...]=total
+    for c in dm_last: c.wait()
+    total=dm_n[0]
+    for k in range(1,8): total=total+dm_n[k]
+    dmod_sum[...]=total
+    for c in stage4: c.wait()
+    cols=pl.ds(pl.multiple_of(head*512,512),512)
+    up_sum[...]=up3[:,cols].astype(f32)+up_z[0].astype(f32)+up_z[1].astype(f32)+up_z[2].astype(f32)
+    down_sum[...]=down3[head].astype(f32)+down_z[0].astype(f32)+down_z[1].astype(f32)+down_z[2].astype(f32)
+    out_sum[...]=out3[head].astype(f32)+out_z[0].astype(f32)+out_z[1].astype(f32)+out_z[2].astype(f32)
+    for c in spread: c.wait()
+    for i in range(4):
+        input_grad[i*part:(i+1)*part,:]=row_all[i].astype(f32)
+    for c in shown: c.wait()
+
+
+def back(queries,do,att,fac,table,xn_one,qkv_full,dy,node_input,modulation,counts,out_rows,up_grad,down_grad,out_grad,dmod,e,scale):
+    rows=queries.shape[0]
+    part=rows//4
+    V=pltpu.VMEM
+    full=pl.BlockSpec(memory_space=V)
+    S=jax.ShapeDtypeStruct
+    copies=3+3+1+4+4+4+1+3+3+7+9+3+3+7
+    return pl.pallas_call(functools.partial(back_kernel,scale),
+        out_shape=(S((rows,512),bf16),S((rows,512),f32),S((64,512),f32),S((64,512),f32),S((16,512),f32),S((64,384),f32),S((8,1024),f32)),
+        in_specs=[full]*10+[pl.BlockSpec(memory_space=pltpu.SMEM)]+[full]*5+[pl.BlockSpec(memory_space=pl.ANY)],
+        out_specs=(full,)*7,
+        scratch_shapes=[V((5,rows,rows),bf16),V((rows,128),f32),V((256,rows),f32),V((5,256,rows),bf16),
+            V((256,rows),bf16),V((256,rows),bf16),V((256,rows),bf16),V((256,rows),bf16),
+            V((rows,384),bf16),V((4,part,512),bf16),V((3,part,512),bf16),V((part,512),bf16),V((4,part,512),bf16),
+            V((4,64,2048),bf16),V((4,4,64,512),bf16),V((4,4,16,512),bf16),
+            V((2,64,2048),bf16),V((4,2,64,512),bf16),V((4,2,16,512),bf16),
+            V((64,2048),bf16),V((4,64,512),bf16),V((4,16,512),bf16),
+            V((3,64,512),bf16),V((3,64,512),bf16),V((3,16,512),bf16),
+            V((8,64,384),bf16),V((7,64,384),bf16),V((4,8,1024),f32),V((8,1024),f32),V((8,8,1024),f32),
+            pltpu.SemaphoreType.DMA((copies,)),pltpu.SemaphoreType.DMA((copies,)),pltpu.SemaphoreType.DMA((5,))],
+        compiler_params=pltpu.CompilerParams(vmem_limit_bytes=62<<20,collective_id=3,has_side_effects=True),
+        name="back")(queries,do,att,fac,table,xn_one,qkv_full,dy,node_input,modulation,counts,out_rows,
+            up_grad.reshape(4,2,64,2048),down_grad.reshape(4,4,2,64,512),out_grad.reshape(4,4,2,16,512),dmod,e)
+
+
+def per_device_near(
+    node_input, cotangent, sigma_embed, neighbours, neighbour_valid, batch_counts, step_count,
+    ada_master, ada_first, ada_second, qkv_master, qkv_first, qkv_second, out_master, out_first, out_second,
+    up_master, up_first, up_second, down_master, down_first, down_second,
+):
+    rows=node_input.shape[0]
+    node=lax.axis_index("node")
+    scale=128**-0.5
+    sigma_part=lax.dynamic_slice_in_dim(sigma_embed,node*64,64,1)
+    hik,lok=slots(neighbours,neighbour_valid,node,rows)
+    att,fac,queries,table,xn_one,modulation,qkv_full,out_full,up_full,down_full,e=front(
+        node_input,sigma_part,ada_master,qkv_master,out_master,up_master,down_master,batch_counts,hik,lok,scale)
+    do,dy,out_rows,up_grad,down_grad,out_grad,dmod=middle(
+        node_input,cotangent,att,modulation,batch_counts,out_full,up_full,down_full)
+    node_output,input_grad,up_sum,down_sum,out_sum,qkv_sum,dmod_sum=back(
+        queries,do,att,fac,table,xn_one,qkv_full,dy,node_input,modulation,batch_counts,out_rows,up_grad,down_grad,out_grad,dmod,e,scale)
+    batch_grad=jnp.concatenate([dmod_sum[:4],dmod_sum[4:]],axis=1)
+    ada_sum=jnp.dot(sigma_part.astype(f32).T,batch_grad,precision=highest)
+    count_value=step_count[0].astype(f32)
+    ada_res=adamw_update(ada_master,ada_first,ada_second,ada_sum,(4*COND)**(-0.5),count_value)
+    qkv_res=adamw_update(qkv_master,qkv_first,qkv_second,qkv_sum,(WIDTH//2)**(-0.5),count_value)
+    out_res=adamw_update(out_master,out_first,out_second,out_sum,(WIDTH//4)**(-0.5),count_value)
+    up_res=adamw_update(up_master,up_first,up_second,up_sum,WIDTH**(-0.5),count_value)
+    down_res=adamw_update(down_master,down_first,down_second,down_sum,HIDDEN_SIZE**(-0.5),count_value)
+    return (node_output,input_grad)+ada_res+qkv_res+out_res+up_res+down_res
 
 
 def per_device(
@@ -352,6 +786,7 @@
 
 
 def solution(mesh):
+    chosen = per_device_near if mesh.shape["node"] == 8 and mesh.shape["head"] == 4 else per_device
     placed = (
         P("node", None),
         P("node", None),
@@ -377,7 +812,7 @@
         P(("head", "node"), None),
     )
     return jax.shard_map(
-        per_device,
+        chosen,
         mesh=mesh,
         in_specs=placed,
         out_specs=(

time: 579 us -> 214 us (0.37); the launches traced: 572 us -> 214 us
  waiting for transfers between devices: 281 us -> 0 us
  Pallas kernels: 56.8 us -> 199 us
  blocking collectives: 113 us -> 0 us
  matrix products: 36.6 us -> 1.91 us
  other arithmetic: 37 us -> 4.64 us
  local copies, waits for them, and re-layouts: 22.8 us -> 6.36 us
  between operations: 15.8 us -> 1.66 us
  starting transfers between devices: 9.08 us -> 0 us
    psum x3 -> x0, waiting for transfers between devices: 181 us -> none  [the longest x1 87.4 us: per_device(): lax.psum(jnp.dot(activated, down_full, preferred_element_type=f32).astype...]
    pallas_call x2 -> x3, Pallas kernels: 56.8 us -> 199 us  [the longest x1 108 us: back(): pl.pallas_call(functools.partial(back_kernel, scale), out_shape=(S((rows,...]
    reduce_scatter x4 -> x0, waiting for transfers between devices: 64.7 us -> none  [the longest x1 34.7 us: per_device(): lax.psum_scatter(down_grad, 'node', scatter_dimension=0, tiled=True)]
    all_gather x4 -> x0, blocking collectives: 64 us -> none  [the longest x1 34.8 us: per_device(): lax.all_gather(out_master.astype(bf16), 'node', axis=0, tiled=True)]
    psum x2 -> x0, blocking collectives: 49.2 us -> none  [the longest x1 25.5 us: per_device(): lax.psum(jnp.dot(sigma_part, ada_master.astype(bf16), preferred_element_t...]
    ppermute x8 -> x0, waiting for transfers between devices: 35.1 us -> none  [passed_along(): return lax.ppermute(block, axis, route)]
    dot_general x16 -> x1, matrix products: 36.6 us -> 1.91 us  [per_device_near(): ada_sum = jnp.dot(sigma_part.astype(f32).T, batch_grad, precision=highest)]
    unnamed x82 -> x49, local copies, waits for them, and re-layouts: 15.9 us -> 4.12 us
  transfers between devices with their start and end apart: 15 -> 0, of which waited for: 8 -> 0; matrix products, arithmetic and copies ran while one was open for 6% -> 0% of each run, Pallas kernels for 3% -> 0%
where the time goes in v2:
time: 214 us
  Pallas kernels  199 us (93%)
  local copies, waits for them, and re-layouts  6.36 us (3%)
  other arithmetic  4.64 us (2%)
    pallas_call x1, Pallas kernels, back(): pl.pallas_call(functools.partial(back_kernel, scale), out_shape=(S((rows,...  108 us
    pallas_call x1, Pallas kernels, front(): pl.pallas_call(functools.partial(front_kernel, scale * math.log2(math.e))...  66.7 us
    pallas_call x1, Pallas kernels, middle(): pl.pallas_call(middle_kernel, out_shape=(S((rows, 128), bf16), S((part, 5...  24.5 us

profile of v2, /device:TPU:0, one launch (start us, length us, event | category | flops | bytes accessed | tf_op | source)
XLA Modules:
  0.0 213.8 jit_solution(4662216983390515185)
XLA Ops:
  0.7 0.0 copy-start
  0.7 0.7 copy-done
  1.3 0.6 constant_dynamic-slice_fusion.sigma
  2.0 1.0 copy.42
  3.0 0.2 reshape.55
  3.3 0.9 broadcast_compare_fusion.1
  4.1 0.3 copy.41
  4.4 0.3 reshape.54
  4.7 0.8 add_select_fusion
  5.5 66.7 %front.1 = (f32[1024,128]{1,0:T(8,128)}, f32[1024,128]{1,0:T(8,128)}, bf16[1024,128]{1,0:T(8,128)(2,1)}, bf16[5,1024,256]{2,1,0:T(8,128)(2,1)}, bf16[1024,512]{1...) custom-call(bf16[1024,512]{1,0:T(8,128)(2,1)} %node_input.5, ...), custom_call_target="tpu_custom_call" | custom-call | tf_op jit(solution)/shard_map/front/pallas_call | solution.py:316
  72.2 24.5 %middle.1 = (bf16[1024,128]{1,0:T(8,128)(2,1)}, f32[256,512]{1,0:T(8,128)}, bf16[256,512]{1,0:T(8,128)(2,1)}, bf16[512,2048]{1,0:T(8,128)(2,1)}, bf16[4,512,512]...) custom-call(bf16[1024,512]{1,0:T(8,128)(2,1)} %node_input.5, bf16[1024,512]{1,0:T(8,128)(2,1)} %cotangent.1, ...), custom_call_target="tpu_custom_call" | custom-call | tf_op jit(solution)/shard_map/middle/pallas_call | solution.py:410
  96.7 0.0 copy-start.5
  96.7 0.0 copy-start.20
  96.8 0.0 copy-start.21
  96.8 0.0 copy-start.22
  96.8 108.0 %back.1 = (bf16[1024,512]{1,0:T(8,128)(2,1)}, f32[1024,512]{1,0:T(8,128)}, f32[64,512]{1,0:T(8,128)}, f32[64,512]{1,0:T(8,128)}, f32[16,512]{1,0:T(8,128)}, /*index=5*/f32[64,384]{1,0:T(8,128)}, f32[8,1024]{1,0:T(8,128)}) custom-call(bf16[1024,128]{1,0:T(8,128)(2,1)} %get-tuple-element.42.queries, bf16[1024,128]{1,0:T(8,128)(2,1)} %get-tuple-element.48.do, ...), custom_call_target="tpu_custom_call" | custom-call | tf_op jit(solution)/shard_map/back/pallas_call | solution.py:573
  204.8 0.8 fusion.22
  206.3 0.0 copy-done.5
  206.3 0.0 copy-done.20
  206.3 0.0 copy-done.21
  206.4 0.0 copy-done.22
  206.4 0.0 copy-start.3
  206.4 0.0 copy-start.8
  206.4 0.0 copy-start.9
  206.4 0.0 copy-start.13
  206.4 0.0 copy-start.4
  206.4 0.0 copy-start.10
  206.4 0.0 copy-start.11
  206.5 0.0 copy-start.12
  206.5 0.0 copy-start.6
  206.5 0.0 copy-start.14
  206.5 0.0 copy-start.15
  206.5 0.0 copy-start.16
  206.5 1.9 multiply_subtract_fusion
  208.4 0.0 copy-start.2
  208.4 0.0 copy-done.3
  208.4 0.0 copy-done.8
  208.5 0.8 multiply_subtract_fusion.2
  209.3 0.0 copy-done.10
  209.3 0.8 multiply_subtract_fusion.1
  210.1 0.7 multiply_subtract_fusion.3
  210.9 0.0 copy-done.18
  210.9 0.0 copy-done.19
  210.9 0.7 multiply_subtract_fusion.4
  211.5 0.0 copy-done.2
  211.5 1.0 copy.46
  212.5 0.0 copy-done.1
  212.5 1.3 copy.47
  (18 shorter events, 0.0 us)
Async XLA Ops:
  0.7 0.7 copy-start
  96.7 109.6 %copy-start.5 = (f32[64,2048]{1,0:T(8,128)S(1)}, f32[64,2048]{1,0:T(8,128)}, u32[]{:S(2)}) copy-start(f32[64,2048]{1,0:T(8,128)} %ada.1) | copy-start | bytes 1572868
  96.7 109.6 %copy-start.20 = (bf16[4,64]{1,0:T(4,128)(2,1)S(1)}, bf16[4,64]{1,0:T(4,128)(2,1)}, u32[]{:S(2)}) copy-start(bf16[4,64]{1,0:T(4,128)(2,1)} %constant_dynamic-slice_fusion.sigma) | copy-start | bytes 1540
  96.8 109.6 %copy-start.21 = (f32[64,2048]{1,0:T(8,128)S(1)}, f32[64,2048]{1,0:T(8,128)}, u32[]{:S(2)}) copy-start(f32[64,2048]{1,0:T(8,128)} %param.31) | copy-start | bytes 1572868
  96.8 109.6 %copy-start.22 = (f32[64,2048]{1,0:T(8,128)S(1)}, f32[64,2048]{1,0:T(8,128)}, u32[]{:S(2)}) copy-start(f32[64,2048]{1,0:T(8,128)} %param.30) | copy-start | bytes 1572868
  206.4 2.1 copy-start.3
  206.4 2.1 copy-start.8
  206.4 2.1 copy-start.9
  206.4 2.1 copy-start.13
  206.4 2.9 %copy-start.4 = (f32[64,512]{1,0:T(8,128)S(1)}, f32[64,512]{1,0:T(8,128)}, u32[]{:S(2)}) copy-start(f32[64,512]{1,0:T(8,128)} %down.1) | copy-start | bytes 393220
  206.4 2.9 %copy-start.10 = (f32[64,512]{1,0:T(8,128)S(1)}, f32[64,512]{1,0:T(8,128)}, u32[]{:S(2)}) copy-start(f32[64,512]{1,0:T(8,128)} %param.43) | copy-start | bytes 393220
  206.4 2.8 %copy-start.11 = (f32[64,512]{1,0:T(8,128)S(1)}, f32[64,512]{1,0:T(8,128)}, u32[]{:S(2)}) copy-start(f32[64,512]{1,0:T(8,128)} %param.42) | copy-start | bytes 393220
  206.5 2.8 %copy-start.12 = (f32[64,512]{1,0:T(8,128)S(1)}, f32[64,512]{1,0:T(8,128)}, u32[]{:S(2)}) copy-start(f32[64,512]{1,0:T(8,128)} %get-tuple-element.66) | copy-start | bytes 393220
  206.5 3.6 %copy-start.6 = (f32[64,384]{1,0:T(8,128)S(1)}, f32[64,384]{1,0:T(8,128)}, u32[]{:S(2)}) copy-start(f32[64,384]{1,0:T(8,128)} %qkv.1) | copy-start | bytes 294916
  206.5 3.6 %copy-start.14 = (f32[64,384]{1,0:T(8,128)S(1)}, f32[64,384]{1,0:T(8,128)}, u32[]{:S(2)}) copy-start(f32[64,384]{1,0:T(8,128)} %param.34) | copy-start | bytes 294916
  206.5 3.6 %copy-start.15 = (f32[64,384]{1,0:T(8,128)S(1)}, f32[64,384]{1,0:T(8,128)}, u32[]{:S(2)}) copy-start(f32[64,384]{1,0:T(8,128)} %param.33) | copy-start | bytes 294916
  206.5 3.6 %copy-start.16 = (f32[64,384]{1,0:T(8,128)S(1)}, f32[64,384]{1,0:T(8,128)}, u32[]{:S(2)}) copy-start(f32[64,384]{1,0:T(8,128)} %get-tuple-element.63) | copy-start | bytes 294916
  208.4 2.4 %copy-start.7 = (f32[16,512]{1,0:T(8,128)S(1)}, f32[16,512]{1,0:T(8,128)}, u32[]{:S(2)}) copy-start(f32[16,512]{1,0:T(8,128)} %out.1) | copy-start | bytes 98308
  208.4 2.4 %copy-start.17 = (f32[16,512]{1,0:T(8,128)S(1)}, f32[16,512]{1,0:T(8,128)}, u32[]{:S(2)}) copy-start(f32[16,512]{1,0:T(8,128)} %param.37) | copy-start | bytes 98308
  208.4 2.4 %copy-start.18 = (f32[16,512]{1,0:T(8,128)S(1)}, f32[16,512]{1,0:T(8,128)}, u32[]{:S(2)}) copy-start(f32[16,512]{1,0:T(8,128)} %param.36) | copy-start | bytes 98308
  208.4 2.4 %copy-start.19 = (f32[16,512]{1,0:T(8,128)S(1)}, f32[16,512]{1,0:T(8,128)}, u32[]{:S(2)}) copy-start(f32[16,512]{1,0:T(8,128)} %get-tuple-element.64) | copy-start | bytes 98308
  208.4 3.1 %copy-start.2 = (bf16[1024,512]{1,0:T(8,128)(2,1)S(1)}, bf16[1024,512]{1,0:T(8,128)(2,1)}, u32[]{:S(2)}) copy-start(bf16[1024,512]{1,0:T(8,128)(2,1)} %get-tuple-element.105) | copy-start | bytes 3145732
  209.3 3.2 %copy-start.1 = (f32[1024,512]{1,0:T(8,128)S(1)}, f32[1024,512]{1,0:T(8,128)}, u32[]{:S(2)}) copy-start(f32[1024,512]{1,0:T(8,128)} %get-tuple-element.106) | copy-start | bytes 6291460
